TPU v7x, 128 devices: a whole 4x4x4 slice. The times are simulated.
128 devices in a mesh: outer: 4 (over x_hi, core), inner: 32 (over y, z, x_lo).
Axes of the slice: x: 4 (x_hi: 2, x_lo: 2; x = x_hi * 2 + x_lo), y: 4, z: 4, core: 2. Of those that a mesh axis runs over, the one named last changes fastest.
Arguments:
- projected: bfloat16 [16384, 12288], P(('outer', 'inner')), may hold values from -6 to 6
- short_filter: bfloat16 [3, 12288], replicated, may hold values from -3.5 to 3.5
- long_filter: bfloat16 [16384, 4096], P(('outer', 'inner')), may hold values from 0 to 0.35
- skip: float32 [4096], replicated, may hold values from 0.1 to 1.9
Outputs:
- mixed: bfloat16 [16384, 4096], P(('outer', 'inner'))
All inputs are finite; a program needn't handle non-finite values.
Results may differ from a plain program's by a relative error of at most 0.0075.
Values may be sent and summed in bfloat16 or wider, within the bound.
No kernel may reach another device: no remote copies, remote signals or barrier semaphores. Data moves between devices by JAX's collectives and lax.ppermute only.
A program may use at most 128 MiB of HBM per device.

v0:
```python
import math

import jax
import jax.numpy as jnp
import numpy as np
from jax import lax
from jax.experimental import pallas as pl
from jax.experimental.pallas import tpu as pltpu
from jax.sharding import PartitionSpec as P

AXES = ("outer", "inner")
F32 = jnp.float32
BF16 = jnp.bfloat16


def turn_table(rows, cols, length):
    product = (np.asarray(rows, np.int64) * np.asarray(cols, np.int64)) % length
    angle = product.astype(np.float32) * np.float32(2.0 * math.pi / length)
    angle = angle.astype(np.float64)
    return np.cos(angle).astype(np.float32), np.sin(angle).astype(np.float32)


def tables(segments, tok):
    half = segments
    blocks = 2 * segments
    transform = blocks * tok
    kb = np.arange(half + 1)
    cos_b, sin_b = turn_table(kb[:, None], np.arange(segments)[None, :], blocks)
    first = np.concatenate([cos_b[:half], cos_b[half:], -sin_b[1:half]], 0)
    weight = np.full((half + 1,), 2.0, np.float32)
    weight[0] = weight[half] = 1.0
    cos_w = cos_b.astype(BF16).astype(np.float32) * weight[:, None]
    sin_w = sin_b.astype(BF16).astype(np.float32) * weight[:, None]
    last = np.concatenate([cos_w[:half], cos_w[half:], -sin_w[1:half]], 0).T
    cos_l, sin_l = turn_table(np.arange(tok)[:, None], np.arange(tok)[None, :], tok)
    forward = np.block([[cos_l, -sin_l], [sin_l, cos_l]])
    backward = np.block([[cos_l, sin_l], [-sin_l, cos_l]])
    turn_cos, turn_sin = turn_table(kb[:, None], np.arange(tok)[None, :], transform)
    return (
        first.astype(BF16),
        forward.astype(BF16),
        backward.astype(BF16),
        last.astype(BF16),
        turn_cos[:half],
        turn_sin[:half],
        turn_cos[half:],
        turn_sin[half:],
    )


def featurized(rows, rim, taps):
    rows = rows.astype(F32)
    rim = rim.astype(F32)
    taps = taps.astype(F32)
    index = lax.broadcasted_iota(jnp.int32, rows.shape, 0)
    back1 = jnp.where(index == 0, rim[1:2], pltpu.roll(rows, 1, 0))
    back2 = pltpu.roll(rows, 2, 0)
    back2 = jnp.where(index == 0, rim[0:1], jnp.where(index == 1, rim[1:2], back2))
    return taps[0:1] * rows + taps[1:2] * back1 + taps[2:3] * back2


def gate_kernel(k_ref, v_ref, rk_ref, rv_ref, wk_ref, wv_ref, f_ref, send_ref, gated_ref):
    gated = featurized(k_ref[...], rk_ref[...], wk_ref[...]) * featurized(
        v_ref[...], rv_ref[...], wv_ref[...]
    )
    gated = gated.astype(BF16)
    gated_ref[...] = gated
    dests, twice, tok = send_ref.shape
    own = twice // 2
    send_ref[:, :own, :] = gated.T.reshape(dests, own, tok)
    send_ref[:, own:, :] = f_ref[...].T.reshape(dests, own, tok)


def gate(projected, rim, short_filter, long_filter, devices):
    tok, width = long_filter.shape
    own = width // devices
    steps = 8
    cols = width // steps
    peers = devices // steps

    def col(third):
        return lambda i: (0, i + third * steps)

    return pl.pallas_call(
        gate_kernel,
        grid=(steps,),
        in_specs=[
            pl.BlockSpec((tok, cols), col(1)),
            pl.BlockSpec((tok, cols), col(2)),
            pl.BlockSpec((rim.shape[0], cols), col(1)),
            pl.BlockSpec((rim.shape[0], cols), col(2)),
            pl.BlockSpec((short_filter.shape[0], cols), col(1)),
            pl.BlockSpec((short_filter.shape[0], cols), col(2)),
            pl.BlockSpec((tok, cols), lambda i: (0, i)),
        ],
        out_specs=[
            pl.BlockSpec((peers, 2 * own, tok), lambda i: (i, 0, 0)),
            pl.BlockSpec((tok, cols), lambda i: (0, i)),
        ],
        out_shape=[
            jax.ShapeDtypeStruct((devices, 2 * own, tok), BF16),
            jax.ShapeDtypeStruct((tok, width), BF16),
        ],
        name="gate",
    )(projected, projected, rim, rim, short_filter, short_filter, long_filter)


def dot(a, b):
    return jnp.dot(a, b, preferred_element_type=F32)


def spectral_kernel(
    z_ref, first_ref, fwd_ref, bwd_ref, last_ref, tc_ref, ts_ref, hc_ref, hs_ref, out_ref,
    rows_ref, spec_ref, half_ref, half_out_ref, conv_ref,
):
    segments, both, tok = z_ref.shape
    own = both // 2
    piece = 16

    def widen(i, carry):
        start = pl.multiple_of(i * piece, piece)
        block = z_ref[pl.ds(start, piece)].astype(F32).reshape(piece * both, tok)
        rows_ref[pl.ds(pl.multiple_of(start * both, piece * both), piece * both), :] = block
        return carry

    lax.fori_loop(0, segments // piece, widen, 0)

    index = lax.broadcasted_iota(jnp.int32, (segments, tok), 0)
    group = 4

    def first_section(i, carry):
        cols = [
            rows_ref[pl.ds(i * group + j, segments, stride=both), :].astype(BF16)
            for j in range(group)
        ]
        out = dot(first_ref[...], jnp.concatenate(cols, 1))
        tc, ts = tc_ref[...], ts_ref[...]
        for j in range(group):
            real = out[:segments, j * tok : (j + 1) * tok]
            imag = out[segments:, j * tok : (j + 1) * tok]
            half_ref[pl.ds(i * group + j, 1), :] = imag[0:1]
            imag = jnp.where(index == 0, 0.0, imag)
            spec_ref[i * group + j, :, :tok] = (real * tc + imag * ts).astype(BF16)
            spec_ref[i * group + j, :, tok:] = (imag * tc - real * ts).astype(BF16)
        return carry

    lax.fori_loop(0, both // group, first_section, 0)

    def product(sig, fil):
        sr, si, fr, fi = sig[:, :tok], sig[:, tok:], fil[:, :tok], fil[:, tok:]
        return jnp.concatenate(
            [(sr * fr - si * fi).astype(BF16), (sr * fi + si * fr).astype(BF16)], 1
        )

    half = half_ref[...]
    hc, hs = hc_ref[...], hs_ref[...]
    half = jnp.concatenate([(half * hc).astype(BF16), (-half * hs).astype(BF16)], 1)
    half = dot(half, fwd_ref[...])
    half = dot(product(half[:own], half[own:]), bwd_ref[...])
    half_out_ref[...] = half[:, :tok] * hc - half[:, tok:] * hs

    scale = 1.0 / (2 * segments * tok)

    def middle(i, carry):
        tc, ts = tc_ref[...], ts_ref[...]
        reals, imags = [], []
        for j in range(2):
            c = i * 2 + j
            sig = dot(spec_ref[c], fwd_ref[...])
            fil = dot(spec_ref[own + c], fwd_ref[...])
            back = dot(product(sig, fil), bwd_ref[...])
            br, bi = back[:, :tok], back[:, tok:]
            imag = jnp.where(index == 0, half_out_ref[pl.ds(c, 1), :], bi * tc + br * ts)
            reals.append((br * tc - bi * ts).astype(BF16))
            imags.append(imag.astype(BF16))
        stacked = jnp.concatenate(
            [jnp.concatenate(reals, 1), jnp.concatenate(imags, 1)], 0
        )
        conv = dot(last_ref[...], stacked) * scale
        for j in range(2):
            conv_ref[pl.ds(i * 2 + j, segments, stride=own), :] = conv[:, j * tok : (j + 1) * tok]
        return carry

    lax.fori_loop(0, own // 2, middle, 0)

    def narrow(i, carry):
        start = pl.multiple_of(i * piece, piece)
        block = conv_ref[pl.ds(pl.multiple_of(start * own, piece * own), piece * own), :]
        out_ref[pl.ds(start, piece)] = block.astype(BF16).reshape(piece, own, tok)
        return carry

    lax.fori_loop(0, segments // piece, narrow, 0)


def spectral(received, consts):
    segments, both, tok = received.shape
    own = both // 2
    return pl.pallas_call(
        spectral_kernel,
        out_shape=jax.ShapeDtypeStruct((segments, own, tok), BF16),
        in_specs=[pl.BlockSpec(memory_space=pltpu.VMEM)] * 9,
        out_specs=pl.BlockSpec(memory_space=pltpu.VMEM),
        scratch_shapes=[
            pltpu.VMEM((segments * both, tok), F32),
            pltpu.VMEM((both, segments, 2 * tok), BF16),
            pltpu.VMEM((both, tok), F32),
            pltpu.VMEM((own, tok), F32),
            pltpu.VMEM((segments * own, tok), F32),
        ],
        name="spectral",
    )(received, *consts)


def mix_kernel(c_ref, q_ref, s_ref, out_ref):
    peers, own, tok = c_ref.shape
    conv = c_ref[...].reshape(peers * own, tok).T.astype(F32)
    out_ref[...] = (q_ref[...] * (conv + s_ref[...])).astype(BF16)


def mix(conv, query, direct):
    devices, own, tok = conv.shape
    width = devices * own
    steps = 8
    cols = width // steps
    wide = pl.BlockSpec((tok, cols), lambda i: (0, i))
    return pl.pallas_call(
        mix_kernel,
        grid=(steps,),
        in_specs=[pl.BlockSpec((devices // steps, own, tok), lambda i: (i, 0, 0)), wide, wide],
        out_specs=wide,
        out_shape=jax.ShapeDtypeStruct((tok, width), BF16),
        name="mix",
    )(conv, query, direct)


def shards(projected, short_filter, long_filter, skip):
    devices = lax.axis_size(AXES)
    tok, width = long_filter.shape
    tap_count = short_filter.shape[0]
    rim_count = tap_count - 1
    consts = tables(devices, tok)
    rim = lax.ppermute(
        projected[tok - rim_count :], AXES, [(i, i + 1) for i in range(devices - 1)]
    )
    send, gated = gate(projected, rim, short_filter, long_filter, devices)
    received = lax.all_to_all(send, AXES, split_axis=0, concat_axis=0, tiled=True)
    extended = jnp.concatenate([rim[:, :width], projected[:, :width]], 0).astype(F32)
    query = jnp.zeros((tok, width), F32)
    for tap in range(tap_count):
        offset = rim_count - tap
        query = query + short_filter[tap, :width].astype(F32) * extended[offset : offset + tok]
    direct = skip[None, :] * gated.astype(F32)
    conv = spectral(received, consts)
    conv = lax.all_to_all(conv, AXES, split_axis=0, concat_axis=0, tiled=True)
    return mix(conv, query, direct)


def solution(mesh):
    in_specs = (P(AXES, None), P(), P(AXES, None), P())
    return jax.shard_map(
        shards, mesh=mesh, in_specs=in_specs, out_specs=P(AXES, None), check_vma=False
    )
```

profile of v0, /device:TPU:1, one launch (start us, length us, event | category | flops | bytes accessed | tf_op | source)
XLA Modules:
  0.0 109.7 jit_solution(15357848861303478732)
XLA Ops:
  0.0 1.0 slice.27
  1.0 3.9 %collective-permute-start = (bf16[2,12288]{1,0:T(2,128)(2,1)S(1)}, bf16[2,12288]{1,0:T(2,128)(2,1)S(1)}, u32[]{:S(2)}, u32[]{:S(2)}) collective-permute-start(bf16[2,12288]{1,0:T(2,128)(2,1)S(1)} %slice.27), channel_id=1, source_target_pairs={{0,1},{1,2},{2,3},{3,4},{4,5},{5,6},{6,7},{7,8},{8,9},{9,10},{10,1... | collective-permute-start | bytes 147464 | tf_op jit(solution)/shard_map/ppermute | solution.py:242
  4.9 8.2 %collective-permute-done.rk_ref.rv_ref = bf16[2,12288]{1,0:T(2,128)(2,1)S(1)} collective-permute-done((bf16[2,12288]{1,0:T(2,128)(2,1)S(1)}, bf16[2,12288]{1,0:T(2,128)(2,1)S(1)}, u32[]{:S(2)}, u32[]{:S(2)}) %collective-permute-start) | collective-permute-done | bytes 49184 | tf_op jit(solution)/shard_map/ppermute | solution.py:242
  13.2 0.0 copy-start.2
  13.2 0.6 copy-done.2
  13.8 7.2 %gate.1 = (bf16[128,64,128]{2,1,0:T(8,128)(2,1)}, bf16[128,4096]{1,0:T(8,128)(2,1)}) custom-call(bf16[128,12288]{1,0:T(8,128)(2,1)} %v_ref.1, bf16[128,12288]{1,0:T(8,128)(2,1)} %v_ref.1, bf16[2,12288]{1,0:T(2,128)(2,1)} %copy-done.2, bf16[2,12288]{1,0:T(2,128)(2,1)} %copy-done.2, bf16[3,12288]{1,0:T(4,128)(2,1)} %wv_ref.1, bf16[3,12288]{1,0:T(4,128)(2,1)} %wv_ref.1, ...), custom_call_target="tpu_custom_call" | custom-call | tf_op jit(solution)/shard_map/gate/pallas_call | solution.py:84
  21.0 0.0 copy-start.1
  21.0 6.6 %all-to-all-start = ((bf16[128,64,128]{2,1,0:T(8,128)(2,1)}), bf16[128,64,128]{2,1,0:T(8,128)(2,1)}, u32[]{:S(2)}, u32[]{:S(2)}) async-start(bf16[128,64,128]{2,1,0:T(8,128)(2,1)} %get-tuple-element.7), calls=%async_computation | async-start | bytes 4194304 | tf_op jit(solution)/shard_map/all_to_all | solution.py:246
  27.6 0.0 slice-start
  27.6 0.0 slice-start.1
  27.7 0.0 copy-done.1
  27.7 1.2 %slice-done = bf16[128,4096]{1,0:T(8,128)(2,1)S(1)} async-done(((bf16[128,12288]{1,0:T(8,128)(2,1)}), bf16[128,4096]{1,0:T(8,128)(2,1)S(1)}, s32[]{:S(2)}) %slice-start) | async-done | bytes 1048600 | tf_op jit(solution)/shard_map/slice | solution.py:247
  28.9 0.0 slice-done.1
  28.9 0.3 maximum_convert_fusion
  29.2 0.0 copy-start.3
  29.2 28.6 %all-to-all-done.z_ref = bf16[128,64,128]{2,1,0:T(8,128)(2,1)} async-done(((bf16[128,64,128]{2,1,0:T(8,128)(2,1)}), bf16[128,64,128]{2,1,0:T(8,128)(2,1)}, u32[]{:S(2)}, u32[]{:S(2)}) %all-to-all-start) | async-done | bytes 2097184 | tf_op jit(solution)/shard_map/all_to_all | solution.py:246
  57.8 20.7 %spectral.1 = bf16[128,32,128]{2,1,0:T(8,128)(2,1)} custom-call(bf16[128,64,128]{2,1,0:T(8,128)(2,1)} %all-to-all-done.z_ref, bf16[256,128]{1,0:T(8,128)(2,1)} %constant.16.clone.first_ref, bf16[256,256]{1,0:T(8,128)(2,1)} %constant.17.clone.fwd_ref, bf16[256,256]{1,0:T(8,128)(2,1)} %constant.18.clone.bwd_ref, bf16[128,256]{1,0:T(8,128)(2,1)} %constant.19.clone.last_ref, ...), custom_call_target="tpu_custom_call" | custom-call | tf_op jit(solution)/shard_map/spectral/pallas_call | solution.py:198
  78.5 4.6 %all-to-all-start.1 = ((bf16[128,32,128]{2,1,0:T(8,128)(2,1)}), bf16[128,32,128]{2,1,0:T(8,128)(2,1)S(1)}, u32[]{:S(2)}, u32[]{:S(2)}) async-start(bf16[128,32,128]{2,1,0:T(8,128)(2,1)} %spectral.1), calls=%async_computation.1 | async-start | bytes 2097152 | tf_op jit(solution)/shard_map/all_to_all | solution.py:254
  83.1 0.0 copy-done.3
  83.1 3.9 %fusion = (f32[128,4096]{1,0:T(8,128)}, f32[128,4096]{1,0:T(8,128)}) fusion(f32[130,4096]{1,0:T(8,128)S(1)} %maximum_convert_fusion, f32[4096]{0:T(1024)S(1)} %bitcast.4, f32[4096]{0:T(1024)S(1)} %bitcast.5, f32[4096]{0:T(1024)S(1)} %bitcast.3, bf16[128,4096]{1,0:T(8,128)(2,1)} %get-tuple-element.8, f32[4096]{0:T(1024)S(1)} %copy-done.3), kind=kLoop, calls=%fused_computation.1 | loop fusion | flops 3670016 | bytes 11599872 | tf_op jit(solution)/shard_map/add | solution.py:251
  87.0 15.4 %all-to-all-done.1.c_ref = bf16[128,32,128]{2,1,0:T(8,128)(2,1)S(1)} async-done(((bf16[128,32,128]{2,1,0:T(8,128)(2,1)}), bf16[128,32,128]{2,1,0:T(8,128)(2,1)S(1)}, u32[]{:S(2)}, u32[]{:S(2)}) %all-to-all-start.1) | async-done | bytes 1048608 | tf_op jit(solution)/shard_map/all_to_all | solution.py:254
  102.4 0.0 copy-start
  102.4 1.0 copy-done
  103.4 6.3 %mix.1 = bf16[128,4096]{1,0:T(8,128)(2,1)} custom-call(bf16[128,32,128]{2,1,0:T(8,128)(2,1)} %copy-done, f32[128,4096]{1,0:T(8,128)} %get-tuple-element.12.q_ref, f32[128,4096]{1,0:T(8,128)} %get-tuple-element.13.s_ref), custom_call_target="tpu_custom_call" | custom-call | tf_op jit(solution)/shard_map/mix/pallas_call | solution.py:226
  (1 shorter events, 0.0 us)
Async XLA Ops:
  1.0 12.2 %collective-permute-start = (bf16[2,12288]{1,0:T(2,128)(2,1)S(1)}, bf16[2,12288]{1,0:T(2,128)(2,1)S(1)}, u32[]{:S(2)}, u32[]{:S(2)}) collective-permute-start(bf16[2,12288]{1,0:T(2,128)(2,1)S(1)} %slice.27), channel_id=1, source_target_pairs={{0,1},{1,2},{2,3},{3,4},{4,5},{5,6},{6,7},{7,8},{8,9},{9,10},{10,1... | collective-permute-start | bytes 147464 | tf_op jit(solution)/shard_map/ppermute | solution.py:242
  13.2 0.6 copy-start.2
  21.0 6.7 %copy-start.1 = (bf16[3,12288]{1,0:T(4,128)(2,1)S(1)}, bf16[3,12288]{1,0:T(4,128)(2,1)}, u32[]{:S(2)}) copy-start(bf16[3,12288]{1,0:T(4,128)(2,1)} %wv_ref.1) | copy-start | bytes 221188
  21.0 36.8 %all-to-all-start = ((bf16[128,64,128]{2,1,0:T(8,128)(2,1)}), bf16[128,64,128]{2,1,0:T(8,128)(2,1)}, u32[]{:S(2)}, u32[]{:S(2)}) async-start(bf16[128,64,128]{2,1,0:T(8,128)(2,1)} %get-tuple-element.7), calls=%async_computation | async-start | bytes 4194304 | tf_op jit(solution)/shard_map/all_to_all | solution.py:246
  27.6 1.2 %slice-start = ((bf16[128,12288]{1,0:T(8,128)(2,1)}), bf16[128,4096]{1,0:T(8,128)(2,1)S(1)}, s32[]{:S(2)}) async-start(bf16[128,12288]{1,0:T(8,128)(2,1)} %v_ref.1), calls=%async_computation.2 | async-start | bytes 2097152 | tf_op jit(solution)/shard_map/slice | solution.py:247
  27.6 1.2 %slice-start.1 = ((bf16[2,12288]{1,0:T(2,128)(2,1)}), bf16[2,4096]{1,0:T(2,128)(2,1)S(1)}, s32[]{:S(2)}) async-start(bf16[2,12288]{1,0:T(2,128)(2,1)} %copy-done.2), calls=%async_computation.3 | async-start | bytes 32768 | tf_op jit(solution)/shard_map/slice | solution.py:247
  29.2 53.9 %copy-start.3 = (f32[4096]{0:T(1024)S(1)}, f32[4096]{0:T(1024)}, u32[]{:S(2)}) copy-start(f32[4096]{0:T(1024)} %param.15) | copy-start | bytes 49156
  78.5 24.0 %all-to-all-start.1 = ((bf16[128,32,128]{2,1,0:T(8,128)(2,1)}), bf16[128,32,128]{2,1,0:T(8,128)(2,1)S(1)}, u32[]{:S(2)}, u32[]{:S(2)}) async-start(bf16[128,32,128]{2,1,0:T(8,128)(2,1)} %spectral.1), calls=%async_computation.1 | async-start | bytes 2097152 | tf_op jit(solution)/shard_map/all_to_all | solution.py:254
  102.4 1.0 copy-start
where the time goes:
time: 110 us
  waiting for transfers between devices  52.3 us (48%)
  Pallas kernels  34.1 us (31%)
  starting transfers between devices  15.2 us (14%)
  other arithmetic  4.26 us (4%)
  local copies, waits for them, and re-layouts  3.73 us (3%)
    all_to_all x1, waiting for transfers between devices, shards(): lax.all_to_all(send, AXES, split_axis=0, concat_axis=0, tiled=True)  28.6 us
    pallas_call x1, Pallas kernels, spectral(): pl.pallas_call(spectral_kernel, out_shape=jax.ShapeDtypeStruct((segments,...  20.7 us
    all_to_all x1, waiting for transfers between devices, shards(): conv = lax.all_to_all(conv, AXES, split_axis=0, concat_axis=0, tiled=True)  15.4 us
    ppermute x1, waiting for transfers between devices, shards(): lax.ppermute(projected[tok - rim_count:], AXES, [(i, i + 1) for i in rang...  8.24 us
    pallas_call x1, Pallas kernels, gate(): pl.pallas_call(gate_kernel, grid=(steps,), in_specs=[pl.BlockSpec((tok, c...  7.2 us
    all_to_all x1, starting transfers between devices, shards(): lax.all_to_all(send, AXES, split_axis=0, concat_axis=0, tiled=True)  6.64 us
    pallas_call x1, Pallas kernels, mix(): pl.pallas_call(mix_kernel, grid=(steps,), in_specs=[pl.BlockSpec((devices...  6.26 us
    all_to_all x1, starting transfers between devices, shards(): conv = lax.all_to_all(conv, AXES, split_axis=0, concat_axis=0, tiled=True)  4.59 us
  transfers between devices with their start and end apart: 3, of which 3 were waited for; matrix products, arithmetic and copies ran while one was open for 4% of the time, Pallas kernels for 0%

commit v1 on v0

--- a/solution.py
+++ b/solution.py
@@ -1,3 +1,4 @@
+import functools
 import math
 
 import jax
@@ -11,6 +12,7 @@
 AXES = ("outer", "inner")
 F32 = jnp.float32
 BF16 = jnp.bfloat16
+PAD = 1
 
 
 def turn_table(rows, cols, length):
@@ -18,6 +20,11 @@
     angle = product.astype(np.float32) * np.float32(2.0 * math.pi / length)
     angle = angle.astype(np.float64)
     return np.cos(angle).astype(np.float32), np.sin(angle).astype(np.float32)
+
+
+def paired(reals, imags):
+    both = np.stack([reals.reshape(-1, 8, reals.shape[1]), imags.reshape(-1, 8, imags.shape[1])], 1)
+    return both.reshape(-1, reals.shape[1])
 
 
 def tables(segments, tok):
@@ -26,12 +33,12 @@
     transform = blocks * tok
     kb = np.arange(half + 1)
     cos_b, sin_b = turn_table(kb[:, None], np.arange(segments)[None, :], blocks)
-    first = np.concatenate([cos_b[:half], cos_b[half:], -sin_b[1:half]], 0)
+    first = paired(cos_b[:half], np.concatenate([cos_b[half:], -sin_b[1:half]], 0))
     weight = np.full((half + 1,), 2.0, np.float32)
     weight[0] = weight[half] = 1.0
     cos_w = cos_b.astype(BF16).astype(np.float32) * weight[:, None]
     sin_w = sin_b.astype(BF16).astype(np.float32) * weight[:, None]
-    last = np.concatenate([cos_w[:half], cos_w[half:], -sin_w[1:half]], 0).T
+    last = np.concatenate([cos_w[:half], cos_w[half:], -sin_w[1:half]], 0).T / transform
     cos_l, sin_l = turn_table(np.arange(tok)[:, None], np.arange(tok)[None, :], tok)
     forward = np.block([[cos_l, -sin_l], [sin_l, cos_l]])
     backward = np.block([[cos_l, sin_l], [-sin_l, cos_l]])
@@ -111,40 +118,54 @@
 
 def spectral_kernel(
     z_ref, first_ref, fwd_ref, bwd_ref, last_ref, tc_ref, ts_ref, hc_ref, hs_ref, out_ref,
-    rows_ref, spec_ref, half_ref, half_out_ref, conv_ref,
+    rows_ref, spec_ref, half_ref, half_out_ref, prod_ref, back_ref, conv_ref,
 ):
     segments, both, tok = z_ref.shape
     own = both // 2
+    pitch = rows_ref.shape[0] // segments
+    out_pitch = conv_ref.shape[0] // segments
     piece = 16
 
     def widen(i, carry):
-        start = pl.multiple_of(i * piece, piece)
-        block = z_ref[pl.ds(start, piece)].astype(F32).reshape(piece * both, tok)
-        rows_ref[pl.ds(pl.multiple_of(start * both, piece * both), piece * both), :] = block
+        for j in range(piece):
+            b = i * piece + j
+            rows_ref[pl.ds(b * pitch, both), :] = z_ref[b].astype(F32)
         return carry
 
     lax.fori_loop(0, segments // piece, widen, 0)
 
-    index = lax.broadcasted_iota(jnp.int32, (segments, tok), 0)
-    group = 4
-
-    def first_section(i, carry):
+    top = 8
+    index = lax.broadcasted_iota(jnp.int32, (top, tok), 0)
+
+    def first_row(row, block):
+        return jnp.concatenate([jnp.where(index == 0, row, block[:top]), block[top:]], 0)
+
+    group, group2, group3, group4 = 16, 16, 16, 32
+
+    run = 16
+
+    def first_section(which, i, carry):
+        start = i * group
+        base = which * own + start
         cols = [
-            rows_ref[pl.ds(i * group + j, segments, stride=both), :].astype(BF16)
+            rows_ref[pl.ds(base + j, segments, stride=pitch), :].astype(BF16)
             for j in range(group)
         ]
         out = dot(first_ref[...], jnp.concatenate(cols, 1))
+        out = out.reshape(segments // top, 2, top, group * tok)
         tc, ts = tc_ref[...], ts_ref[...]
         for j in range(group):
-            real = out[:segments, j * tok : (j + 1) * tok]
-            imag = out[segments:, j * tok : (j + 1) * tok]
-            half_ref[pl.ds(i * group + j, 1), :] = imag[0:1]
-            imag = jnp.where(index == 0, 0.0, imag)
-            spec_ref[i * group + j, :, :tok] = (real * tc + imag * ts).astype(BF16)
-            spec_ref[i * group + j, :, tok:] = (imag * tc - real * ts).astype(BF16)
-        return carry
-
-    lax.fori_loop(0, both // group, first_section, 0)
+            real = out[:, 0, :, j * tok : (j + 1) * tok].reshape(segments, tok)
+            imag = out[:, 1, :, j * tok : (j + 1) * tok].reshape(segments, tok)
+            half_ref[pl.ds(base + j, 1), :] = imag[0:1]
+            imag = first_row(0.0, imag)
+            both_parts = jnp.concatenate([real * tc + imag * ts, imag * tc - real * ts], 1)
+            both_parts = both_parts.astype(BF16).reshape(segments // run, run, 2 * tok)
+            spec_ref[start + j, :, which] = both_parts
+        return carry
+
+    for which in range(2):
+        lax.fori_loop(0, own // group, functools.partial(first_section, which), 0)
 
     def product(sig, fil):
         sr, si, fr, fi = sig[:, :tok], sig[:, tok:], fil[:, :tok], fil[:, tok:]
@@ -159,34 +180,49 @@
     half = dot(product(half[:own], half[own:]), bwd_ref[...])
     half_out_ref[...] = half[:, :tok] * hc - half[:, tok:] * hs
 
-    scale = 1.0 / (2 * segments * tok)
-
-    def middle(i, carry):
+    def multiply(i, carry):
+        start = i * group2
+        spec = spec_ref[pl.ds(start, group2)].reshape(group2 * 2 * segments, 2 * tok)
+        spec = dot(spec, fwd_ref[...]).reshape(group2 * segments // run, 2, run, 2 * tok)
+        sig = spec[:, 0].reshape(group2 * segments, 2 * tok)
+        fil = spec[:, 1].reshape(group2 * segments, 2 * tok)
+        prod_ref[pl.ds(start, group2)] = product(sig, fil).reshape(group2, segments, 2 * tok)
+        return carry
+
+    lax.fori_loop(0, own // group2, multiply, 0)
+
+    def invert(i, carry):
+        start = i * group3
         tc, ts = tc_ref[...], ts_ref[...]
-        reals, imags = [], []
-        for j in range(2):
-            c = i * 2 + j
-            sig = dot(spec_ref[c], fwd_ref[...])
-            fil = dot(spec_ref[own + c], fwd_ref[...])
-            back = dot(product(sig, fil), bwd_ref[...])
-            br, bi = back[:, :tok], back[:, tok:]
-            imag = jnp.where(index == 0, half_out_ref[pl.ds(c, 1), :], bi * tc + br * ts)
-            reals.append((br * tc - bi * ts).astype(BF16))
-            imags.append(imag.astype(BF16))
-        stacked = jnp.concatenate(
-            [jnp.concatenate(reals, 1), jnp.concatenate(imags, 1)], 0
+        back = dot(
+            prod_ref[pl.ds(start, group3)].reshape(group3 * segments, 2 * tok), bwd_ref[...]
         )
-        conv = dot(last_ref[...], stacked) * scale
-        for j in range(2):
-            conv_ref[pl.ds(i * 2 + j, segments, stride=own), :] = conv[:, j * tok : (j + 1) * tok]
-        return carry
-
-    lax.fori_loop(0, own // 2, middle, 0)
+        for j in range(group3):
+            br = back[j * segments : (j + 1) * segments, :tok]
+            bi = back[j * segments : (j + 1) * segments, tok:]
+            imag = first_row(half_out_ref[pl.ds(start + j, 1), :], bi * tc + br * ts)
+            back_ref[start + j, :segments] = (br * tc - bi * ts).astype(BF16)
+            back_ref[start + j, segments:] = imag.astype(BF16)
+        return carry
+
+    lax.fori_loop(0, own // group3, invert, 0)
+
+    def finish(i, carry):
+        start = i * group4
+        stacked = jnp.concatenate([back_ref[start + j] for j in range(group4)], 1)
+        conv = dot(last_ref[...], stacked)
+        for j in range(group4):
+            conv_ref[pl.ds(start + j, segments, stride=out_pitch), :] = conv[
+                :, j * tok : (j + 1) * tok
+            ]
+        return carry
+
+    lax.fori_loop(0, own // group4, finish, 0)
 
     def narrow(i, carry):
-        start = pl.multiple_of(i * piece, piece)
-        block = conv_ref[pl.ds(pl.multiple_of(start * own, piece * own), piece * own), :]
-        out_ref[pl.ds(start, piece)] = block.astype(BF16).reshape(piece, own, tok)
+        for j in range(piece):
+            b = i * piece + j
+            out_ref[b] = conv_ref[pl.ds(b * out_pitch, own), :].astype(BF16)
         return carry
 
     lax.fori_loop(0, segments // piece, narrow, 0)
@@ -201,11 +237,13 @@
         in_specs=[pl.BlockSpec(memory_space=pltpu.VMEM)] * 9,
         out_specs=pl.BlockSpec(memory_space=pltpu.VMEM),
         scratch_shapes=[
-            pltpu.VMEM((segments * both, tok), F32),
-            pltpu.VMEM((both, segments, 2 * tok), BF16),
+            pltpu.VMEM((segments * (both + PAD), tok), F32),
+            pltpu.VMEM((own, segments // 16, 2, 16, 2 * tok), BF16),
             pltpu.VMEM((both, tok), F32),
             pltpu.VMEM((own, tok), F32),
-            pltpu.VMEM((segments * own, tok), F32),
+            pltpu.VMEM((own, segments, 2 * tok), BF16),
+            pltpu.VMEM((own, 2 * segments, tok), BF16),
+            pltpu.VMEM((segments * (own + PAD), tok), F32),
         ],
         name="spectral",
     )(received, *consts)

time: 110 us -> 97.6 us (0.89)
  Pallas kernels: 34.1 us -> 21.4 us
    pallas_call x1, Pallas kernels: 20.7 us -> 7.9 us  [spectral(): pl.pallas_call(spectral_kernel, out_shape=jax.ShapeDtypeStruct((segments,...]
where the time goes in v1:
time: 97.6 us; the launch traced here: 96.9 us
  waiting for transfers between devices  52.3 us (54%)
  Pallas kernels  21.4 us (22%)
  starting transfers between devices  15.2 us (16%)
  other arithmetic  4.26 us (4%)
  local copies, waits for them, and re-layouts  3.73 us (4%)
    all_to_all x1, waiting for transfers between devices, shards(): lax.all_to_all(send, AXES, split_axis=0, concat_axis=0, tiled=True)  28.6 us
    all_to_all x1, waiting for transfers between devices, shards(): conv = lax.all_to_all(conv, AXES, split_axis=0, concat_axis=0, tiled=True)  15.4 us
    ppermute x1, waiting for transfers between devices, shards(): lax.ppermute(projected[tok - rim_count:], AXES, [(i, i + 1) for i in rang...  8.24 us
    pallas_call x1, Pallas kernels, spectral(): pl.pallas_call(spectral_kernel, out_shape=jax.ShapeDtypeStruct((segments,...  7.9 us
    pallas_call x1, Pallas kernels, gate(): pl.pallas_call(gate_kernel, grid=(steps,), in_specs=[pl.BlockSpec((tok, c...  7.2 us
    all_to_all x1, starting transfers between devices, shards(): lax.all_to_all(send, AXES, split_axis=0, concat_axis=0, tiled=True)  6.64 us
    pallas_call x1, Pallas kernels, mix(): pl.pallas_call(mix_kernel, grid=(steps,), in_specs=[pl.BlockSpec((devices...  6.26 us
    all_to_all x1, starting transfers between devices, shards(): conv = lax.all_to_all(conv, AXES, split_axis=0, concat_axis=0, tiled=True)  4.59 us
  transfers between devices with their start and end apart: 3, of which 3 were waited for; matrix products, arithmetic and copies ran while one was open for 4% of the time, Pallas kernels for 0%

profile of v1, /device:TPU:1, one launch (start us, length us, event | category | flops | bytes accessed | tf_op | source)
XLA Modules:
  0.0 96.9 jit_solution(15620385169062850150)
XLA Ops:
  0.0 1.0 %slice.27 = bf16[2,12288]{1,0:T(2,128)(2,1)S(1)} slice(bf16[128,12288]{1,0:T(8,128)(2,1)} %v_ref.1), slice={[126:128], [0:12288]} | slice | bytes 98304 | tf_op jit(solution)/shard_map/slice | solution.py:281
  1.0 3.9 %collective-permute-start = (bf16[2,12288]{1,0:T(2,128)(2,1)S(1)}, bf16[2,12288]{1,0:T(2,128)(2,1)S(1)}, u32[]{:S(2)}, u32[]{:S(2)}) collective-permute-start(bf16[2,12288]{1,0:T(2,128)(2,1)S(1)} %slice.27), channel_id=1, source_target_pairs={{0,1},{1,2},{2,3},{3,4},{4,5},{5,6},{6,7},{7,8},{8,9},{9,10},{10,1... | collective-permute-start | bytes 147464 | tf_op jit(solution)/shard_map/ppermute | solution.py:280
  4.9 8.2 %collective-permute-done.rk_ref.rv_ref = bf16[2,12288]{1,0:T(2,128)(2,1)S(1)} collective-permute-done((bf16[2,12288]{1,0:T(2,128)(2,1)S(1)}, bf16[2,12288]{1,0:T(2,128)(2,1)S(1)}, u32[]{:S(2)}, u32[]{:S(2)}) %collective-permute-start) | collective-permute-done | bytes 49184 | tf_op jit(solution)/shard_map/ppermute | solution.py:280
  13.2 0.0 copy-start.2
  13.2 0.6 copy-done.2
  13.8 7.2 %gate.1 = (bf16[128,64,128]{2,1,0:T(8,128)(2,1)}, bf16[128,4096]{1,0:T(8,128)(2,1)}) custom-call(bf16[128,12288]{1,0:T(8,128)(2,1)} %v_ref.1, bf16[128,12288]{1,0:T(8,128)(2,1)} %v_ref.1, bf16[2,12288]{1,0:T(2,128)(2,1)} %copy-done.2, bf16[2,12288]{1,0:T(2,128)(2,1)} %copy-done.2, bf16[3,12288]{1,0:T(4,128)(2,1)} %wv_ref.1, bf16[3,12288]{1,0:T(4,128)(2,1)} %wv_ref.1, ...), custom_call_target="tpu_custom_call" | custom-call | tf_op jit(solution)/shard_map/gate/pallas_call | solution.py:91
  21.0 0.0 copy-start.1
  21.0 6.6 %all-to-all-start = ((bf16[128,64,128]{2,1,0:T(8,128)(2,1)}), bf16[128,64,128]{2,1,0:T(8,128)(2,1)}, u32[]{:S(2)}, u32[]{:S(2)}) async-start(bf16[128,64,128]{2,1,0:T(8,128)(2,1)} %get-tuple-element.7), calls=%async_computation | async-start | bytes 4194304 | tf_op jit(solution)/shard_map/all_to_all | solution.py:284
  27.6 0.0 slice-start
  27.6 0.0 slice-start.1
  27.7 0.0 copy-done.1
  27.7 1.2 %slice-done = bf16[128,4096]{1,0:T(8,128)(2,1)S(1)} async-done(((bf16[128,12288]{1,0:T(8,128)(2,1)}), bf16[128,4096]{1,0:T(8,128)(2,1)S(1)}, s32[]{:S(2)}) %slice-start) | async-done | bytes 1048600 | tf_op jit(solution)/shard_map/slice | solution.py:285
  28.9 0.0 slice-done.1
  28.9 0.3 maximum_convert_fusion
  29.2 0.0 copy-start.3
  29.2 28.6 %all-to-all-done.z_ref = bf16[128,64,128]{2,1,0:T(8,128)(2,1)} async-done(((bf16[128,64,128]{2,1,0:T(8,128)(2,1)}), bf16[128,64,128]{2,1,0:T(8,128)(2,1)}, u32[]{:S(2)}, u32[]{:S(2)}) %all-to-all-start) | async-done | bytes 2097184 | tf_op jit(solution)/shard_map/all_to_all | solution.py:284
  57.8 7.9 %spectral.1 = bf16[128,32,128]{2,1,0:T(8,128)(2,1)} custom-call(bf16[128,64,128]{2,1,0:T(8,128)(2,1)} %all-to-all-done.z_ref, bf16[256,128]{1,0:T(8,128)(2,1)} %constant.16.clone.first_ref, bf16[256,256]{1,0:T(8,128)(2,1)} %constant.17.clone.fwd_ref, bf16[256,256]{1,0:T(8,128)(2,1)} %constant.18.clone.bwd_ref, bf16[128,256]{1,0:T(8,128)(2,1)} %constant.19.clone.last_ref, ...), custom_call_target="tpu_custom_call" | custom-call | tf_op jit(solution)/shard_map/spectral/pallas_call | solution.py:234
  65.7 4.6 %all-to-all-start.1 = ((bf16[128,32,128]{2,1,0:T(8,128)(2,1)}), bf16[128,32,128]{2,1,0:T(8,128)(2,1)S(1)}, u32[]{:S(2)}, u32[]{:S(2)}) async-start(bf16[128,32,128]{2,1,0:T(8,128)(2,1)} %spectral.1), calls=%async_computation.1 | async-start | bytes 2097152 | tf_op jit(solution)/shard_map/all_to_all | solution.py:292
  70.3 0.0 copy-done.3
  70.3 3.9 %fusion = (f32[128,4096]{1,0:T(8,128)}, f32[128,4096]{1,0:T(8,128)}) fusion(f32[130,4096]{1,0:T(8,128)S(1)} %maximum_convert_fusion, f32[4096]{0:T(1024)S(1)} %bitcast.4, f32[4096]{0:T(1024)S(1)} %bitcast.5, f32[4096]{0:T(1024)S(1)} %bitcast.3, bf16[128,4096]{1,0:T(8,128)(2,1)} %get-tuple-element.8, f32[4096]{0:T(1024)S(1)} %copy-done.3), kind=kLoop, calls=%fused_computation.1 | loop fusion | flops 3670016 | bytes 11599872 | tf_op jit(solution)/shard_map/add | solution.py:289
  74.2 15.4 %all-to-all-done.1.c_ref = bf16[128,32,128]{2,1,0:T(8,128)(2,1)S(1)} async-done(((bf16[128,32,128]{2,1,0:T(8,128)(2,1)}), bf16[128,32,128]{2,1,0:T(8,128)(2,1)S(1)}, u32[]{:S(2)}, u32[]{:S(2)}) %all-to-all-start.1) | async-done | bytes 1048608 | tf_op jit(solution)/shard_map/all_to_all | solution.py:292
  89.7 0.0 copy-start
  89.7 1.0 %copy-done = bf16[128,32,128]{2,1,0:T(8,128)(2,1)} copy-done((bf16[128,32,128]{2,1,0:T(8,128)(2,1)}, bf16[128,32,128]{2,1,0:T(8,128)(2,1)S(1)}, u32[]{:S(2)}) %copy-start) | copy-done | bytes 1048600
  90.6 6.3 %mix.1 = bf16[128,4096]{1,0:T(8,128)(2,1)} custom-call(bf16[128,32,128]{2,1,0:T(8,128)(2,1)} %copy-done, f32[128,4096]{1,0:T(8,128)} %get-tuple-element.12.q_ref, f32[128,4096]{1,0:T(8,128)} %get-tuple-element.13.s_ref), custom_call_target="tpu_custom_call" | custom-call | tf_op jit(solution)/shard_map/mix/pallas_call | solution.py:264
  (1 shorter events, 0.0 us)
Async XLA Ops:
  1.0 12.2 %collective-permute-start = (bf16[2,12288]{1,0:T(2,128)(2,1)S(1)}, bf16[2,12288]{1,0:T(2,128)(2,1)S(1)}, u32[]{:S(2)}, u32[]{:S(2)}) collective-permute-start(bf16[2,12288]{1,0:T(2,128)(2,1)S(1)} %slice.27), channel_id=1, source_target_pairs={{0,1},{1,2},{2,3},{3,4},{4,5},{5,6},{6,7},{7,8},{8,9},{9,10},{10,1... | collective-permute-start | bytes 147464 | tf_op jit(solution)/shard_map/ppermute | solution.py:280
  13.2 0.6 copy-start.2
  21.0 6.7 %copy-start.1 = (bf16[3,12288]{1,0:T(4,128)(2,1)S(1)}, bf16[3,12288]{1,0:T(4,128)(2,1)}, u32[]{:S(2)}) copy-start(bf16[3,12288]{1,0:T(4,128)(2,1)} %wv_ref.1) | copy-start | bytes 221188
  21.0 36.8 %all-to-all-start = ((bf16[128,64,128]{2,1,0:T(8,128)(2,1)}), bf16[128,64,128]{2,1,0:T(8,128)(2,1)}, u32[]{:S(2)}, u32[]{:S(2)}) async-start(bf16[128,64,128]{2,1,0:T(8,128)(2,1)} %get-tuple-element.7), calls=%async_computation | async-start | bytes 4194304 | tf_op jit(solution)/shard_map/all_to_all | solution.py:284
  27.6 1.2 %slice-start = ((bf16[128,12288]{1,0:T(8,128)(2,1)}), bf16[128,4096]{1,0:T(8,128)(2,1)S(1)}, s32[]{:S(2)}) async-start(bf16[128,12288]{1,0:T(8,128)(2,1)} %v_ref.1), calls=%async_computation.2 | async-start | bytes 2097152 | tf_op jit(solution)/shard_map/slice | solution.py:285
  27.6 1.2 %slice-start.1 = ((bf16[2,12288]{1,0:T(2,128)(2,1)}), bf16[2,4096]{1,0:T(2,128)(2,1)S(1)}, s32[]{:S(2)}) async-start(bf16[2,12288]{1,0:T(2,128)(2,1)} %copy-done.2), calls=%async_computation.3 | async-start | bytes 32768 | tf_op jit(solution)/shard_map/slice | solution.py:285
  29.2 41.1 %copy-start.3 = (f32[4096]{0:T(1024)S(1)}, f32[4096]{0:T(1024)}, u32[]{:S(2)}) copy-start(f32[4096]{0:T(1024)} %param.15) | copy-start | bytes 49156
  65.7 24.0 %all-to-all-start.1 = ((bf16[128,32,128]{2,1,0:T(8,128)(2,1)}), bf16[128,32,128]{2,1,0:T(8,128)(2,1)S(1)}, u32[]{:S(2)}, u32[]{:S(2)}) async-start(bf16[128,32,128]{2,1,0:T(8,128)(2,1)} %spectral.1), calls=%async_computation.1 | async-start | bytes 2097152 | tf_op jit(solution)/shard_map/all_to_all | solution.py:292
  89.7 1.0 %copy-start = (bf16[128,32,128]{2,1,0:T(8,128)(2,1)}, bf16[128,32,128]{2,1,0:T(8,128)(2,1)S(1)}, u32[]{:S(2)}) copy-start(bf16[128,32,128]{2,1,0:T(8,128)(2,1)S(1)} %all-to-all-done.1.c_ref) | copy-start | bytes 3145732

commit v2 on v1

--- a/solution.py
+++ b/solution.py
@@ -233,7 +233,7 @@
     own = both // 2
     return pl.pallas_call(
         spectral_kernel,
-        out_shape=jax.ShapeDtypeStruct((segments, own, tok), BF16),
+        out_shape=pltpu.VMEM((segments, own, tok), BF16),
         in_specs=[pl.BlockSpec(memory_space=pltpu.VMEM)] * 9,
         out_specs=pl.BlockSpec(memory_space=pltpu.VMEM),
         scratch_shapes=[
@@ -245,30 +245,45 @@
             pltpu.VMEM((own, 2 * segments, tok), BF16),
             pltpu.VMEM((segments * (own + PAD), tok), F32),
         ],
+        compiler_params=pltpu.CompilerParams(vmem_limit_bytes=28 << 20),
         name="spectral",
-    )(received, *consts)
-
-
-def mix_kernel(c_ref, q_ref, s_ref, out_ref):
+    )(resident(received), *consts)
+
+
+def mix_kernel(c_ref, q_ref, s_ref, out_ref, sem):
     peers, own, tok = c_ref.shape
-    conv = c_ref[...].reshape(peers * own, tok).T.astype(F32)
-    out_ref[...] = (q_ref[...] * (conv + s_ref[...])).astype(BF16)
+    steps = 8
+    peers = peers // steps
+    cols = peers * own
+
+    def run(buf_ref):
+        for i in range(steps):
+            conv = c_ref[i * peers : (i + 1) * peers].reshape(cols, tok).T.astype(F32)
+            at = pl.ds(i * cols, cols)
+            buf_ref[:, at] = (q_ref[:, at] * (conv + s_ref[:, at])).astype(BF16)
+            pltpu.make_async_copy(buf_ref.at[:, at], out_ref.at[:, at], sem.at[i]).start()
+        for i in range(steps):
+            at = pl.ds(i * cols, cols)
+            pltpu.make_async_copy(buf_ref.at[:, at], out_ref.at[:, at], sem.at[i]).wait()
+
+    pl.run_scoped(run, pltpu.VMEM(out_ref.shape, BF16))
+
+
+def resident(value):
+    return pltpu.with_memory_space_constraint(value, pltpu.VMEM)
 
 
 def mix(conv, query, direct):
     devices, own, tok = conv.shape
-    width = devices * own
-    steps = 8
-    cols = width // steps
-    wide = pl.BlockSpec((tok, cols), lambda i: (0, i))
     return pl.pallas_call(
         mix_kernel,
-        grid=(steps,),
-        in_specs=[pl.BlockSpec((devices // steps, own, tok), lambda i: (i, 0, 0)), wide, wide],
-        out_specs=wide,
-        out_shape=jax.ShapeDtypeStruct((tok, width), BF16),
+        in_specs=[pl.BlockSpec(memory_space=pltpu.VMEM)] * 3,
+        out_specs=pl.BlockSpec(memory_space=pl.ANY),
+        out_shape=jax.ShapeDtypeStruct((tok, devices * own), BF16),
+        scratch_shapes=[pltpu.SemaphoreType.DMA((8,))],
+        compiler_params=pltpu.CompilerParams(vmem_limit_bytes=6 << 20),
         name="mix",
-    )(conv, query, direct)
+    )(resident(conv), resident(query), resident(direct))
 
 
 def shards(projected, short_filter, long_filter, skip):

time: 97.6 us -> 91.5 us (0.938)
  Pallas kernels: 21.4 us -> 14.9 us
  other arithmetic: 4.26 us -> 7.22 us
  waiting for transfers between devices: 52.3 us -> 49.7 us
    pallas_call x2, Pallas kernels: 14.2 us -> 7.64 us  [the longest x1 6.19 us: spectral(): pl.pallas_call(spectral_kernel, out_shape=pltpu.VMEM((segments, own, tok)...]
    all_to_all x1, waiting for transfers between devices: 15.4 us -> 13.9 us  [shards(): conv = lax.all_to_all(conv, AXES, split_axis=0, concat_axis=0, tiled=True)]
    add x1, other arithmetic: 3.93 us -> 5.49 us  [shards(): query + short_filter[tap, :width].astype(F32) * extended[offset:offset +...]
    convert_element_type x1, other arithmetic: 0.29 us -> 1.69 us  [shards(): jnp.concatenate([rim[:, :width], projected[:, :width]], 0).astype(F32)]
    all_to_all x1, waiting for transfers between devices: 28.6 us -> 27.6 us  [shards(): lax.all_to_all(send, AXES, split_axis=0, concat_axis=0, tiled=True)]
    unnamed x8 -> x24, local copies, waits for them, and re-layouts: 1.59 us -> 2.27 us
  transfers between devices with their start and end apart: 3 -> 3, of which waited for: 3 -> 3; matrix products, arithmetic and copies ran while one was open for 4% -> 8% of each run, Pallas kernels for 0% -> 0%
where the time goes in v2:
time: 91.5 us; the launch traced here: 91 us
  waiting for transfers between devices  49.7 us (54%)
  Pallas kernels  14.9 us (16%)
  starting transfers between devices  14.7 us (16%)
  other arithmetic  7.22 us (8%)
  local copies, waits for them, and re-layouts  4.31 us (5%)
    all_to_all x1, waiting for transfers between devices, shards(): lax.all_to_all(send, AXES, split_axis=0, concat_axis=0, tiled=True)  27.6 us
    all_to_all x1, waiting for transfers between devices, shards(): conv = lax.all_to_all(conv, AXES, split_axis=0, concat_axis=0, tiled=True)  13.9 us
    ppermute x1, waiting for transfers between devices, shards(): lax.ppermute(projected[tok - rim_count:], AXES, [(i, i + 1) for i in rang...  8.24 us
    pallas_call x1, Pallas kernels, gate(): pl.pallas_call(gate_kernel, grid=(steps,), in_specs=[pl.BlockSpec((tok, c...  7.21 us
    pallas_call x1, Pallas kernels, spectral(): pl.pallas_call(spectral_kernel, out_shape=pltpu.VMEM((segments, own, tok)...  6.19 us
    all_to_all x1, starting transfers between devices, shards(): lax.all_to_all(send, AXES, split_axis=0, concat_axis=0, tiled=True)  6.18 us
    add x1, other arithmetic, shards(): query + short_filter[tap, :width].astype(F32) * extended[offset:offset +...  5.49 us
    all_to_all x1, starting transfers between devices, shards(): conv = lax.all_to_all(conv, AXES, split_axis=0, concat_axis=0, tiled=True)  4.58 us
  transfers between devices with their start and end apart: 3, of which 3 were waited for; matrix products, arithmetic and copies ran while one was open for 8% of the time, Pallas kernels for 0%

profile of v2, /device:TPU:1, one launch (start us, length us, event | category | flops | bytes accessed | tf_op | source)
XLA Modules:
  0.0 91.0 jit_solution(15558263237424089214)
XLA Ops:
  0.0 1.0 %slice.27 = bf16[2,12288]{1,0:T(2,128)(2,1)S(1)} slice(bf16[128,12288]{1,0:T(8,128)(2,1)} %v_ref.1), slice={[126:128], [0:12288]} | slice | bytes 98304 | tf_op jit(solution)/shard_map/slice | solution.py:296
  1.0 3.9 %collective-permute-start = (bf16[2,12288]{1,0:T(2,128)(2,1)S(1)}, bf16[2,12288]{1,0:T(2,128)(2,1)S(1)}, u32[]{:S(2)}, u32[]{:S(2)}) collective-permute-start(bf16[2,12288]{1,0:T(2,128)(2,1)S(1)} %slice.27), channel_id=1, source_target_pairs={{0,1},{1,2},{2,3},{3,4},{4,5},{5,6},{6,7},{7,8},{8,9},{9,10},{10,1... | collective-permute-start | bytes 147464 | tf_op jit(solution)/shard_map/ppermute | solution.py:295
  4.9 8.2 %collective-permute-done.rk_ref.rv_ref = bf16[2,12288]{1,0:T(2,128)(2,1)S(1)} collective-permute-done((bf16[2,12288]{1,0:T(2,128)(2,1)S(1)}, bf16[2,12288]{1,0:T(2,128)(2,1)S(1)}, u32[]{:S(2)}, u32[]{:S(2)}) %collective-permute-start) | collective-permute-done | bytes 49184 | tf_op jit(solution)/shard_map/ppermute | solution.py:295
  13.2 0.0 copy-start.10
  13.2 0.6 copy-done.10
  13.8 7.2 %gate.1 = (bf16[128,64,128]{2,1,0:T(8,128)(2,1)}, bf16[128,4096]{1,0:T(8,128)(2,1)}) custom-call(bf16[128,12288]{1,0:T(8,128)(2,1)} %v_ref.1, bf16[128,12288]{1,0:T(8,128)(2,1)} %v_ref.1, bf16[2,12288]{1,0:T(2,128)(2,1)} %copy-done.10, bf16[2,12288]{1,0:T(2,128)(2,1)} %copy-done.10, bf16[3,12288]{1,0:T(4,128)(2,1)} %wv_ref.1, bf16[3,12288]{1,0:T(4,128)(2,1)} %wv_ref.1, ...), custom_call_target="tpu_custom_call" | custom-call | tf_op jit(solution)/shard_map/gate/pallas_call | solution.py:91
  21.0 0.0 copy-start.9
  21.0 6.2 %all-to-all-start = ((bf16[128,64,128]{2,1,0:T(8,128)(2,1)}), bf16[128,64,128]{2,1,0:T(8,128)(2,1)S(1)}, u32[]{:S(2)}, u32[]{:S(2)}) async-start(bf16[128,64,128]{2,1,0:T(8,128)(2,1)} %get-tuple-element.7), calls=%async_computation | async-start | bytes 4194304 | tf_op jit(solution)/shard_map/all_to_all | solution.py:299
  27.2 0.0 slice-start
  27.2 0.0 slice-start.1
  27.2 0.0 copy-done.9
  27.2 0.0 copy-start.1
  27.2 0.0 copy-start.2
  27.3 0.0 copy-start.3
  27.3 0.0 copy-start.4
  27.3 0.0 copy-start.5
  27.3 0.0 copy-start.6
  27.3 0.0 copy-start.7
  27.3 0.0 copy-start.8
  27.4 1.1 %slice-done = bf16[128,4096]{1,0:T(8,128)(2,1)S(1)} async-done(((bf16[128,12288]{1,0:T(8,128)(2,1)}), bf16[128,4096]{1,0:T(8,128)(2,1)S(1)}, s32[]{:S(2)}) %slice-start) | async-done | bytes 1048600 | tf_op jit(solution)/shard_map/slice | solution.py:300
  28.4 0.0 slice-done.1
  28.4 1.7 %maximum_convert_fusion = f32[130,4096]{1,0:T(8,128)} fusion(bf16[128,4096]{1,0:T(8,128)(2,1)S(1)} %slice-done, bf16[2,4096]{1,0:T(2,128)(2,1)S(1)} %slice-done.1), kind=kLoop, calls=%fused_computation.6 | loop fusion | flops 2129920 | bytes 3194880 | tf_op jit(solution)/shard_map/convert_element_type | solution.py:300
  30.1 0.0 copy-start.11
  30.1 27.6 %all-to-all-done.z_ref = bf16[128,64,128]{2,1,0:T(8,128)(2,1)S(1)} async-done(((bf16[128,64,128]{2,1,0:T(8,128)(2,1)}), bf16[128,64,128]{2,1,0:T(8,128)(2,1)S(1)}, u32[]{:S(2)}, u32[]{:S(2)}) %all-to-all-start) | async-done | bytes 2097184 | tf_op jit(solution)/shard_map/all_to_all | solution.py:299
  57.7 0.0 copy-done.1
  57.7 0.0 copy-done.2
  57.7 0.0 copy-done.3
  57.7 0.0 copy-done.4
  57.7 0.0 copy-done.5
  57.7 0.0 copy-done.6
  57.7 0.0 copy-done.7
  57.7 0.0 copy-done.8
  57.7 6.2 %spectral.1 = bf16[128,32,128]{2,1,0:T(8,128)(2,1)} custom-call(bf16[128,64,128]{2,1,0:T(8,128)(2,1)S(1)} %all-to-all-done.z_ref, bf16[256,128]{1,0:T(8,128)(2,1)S(1)} %copy-done.6, bf16[256,256]{1,0:T(8,128)(2,1)S(1)} %copy-done.2, bf16[256,256]{1,0:T(8,128)(2,1)S(1)} %copy-done.1, bf16[128,256]{1,0:T(8,128)(2,1)S(1)} %copy-done.5, ...), custom_call_target="tpu_custom_call" | custom-call | tf_op jit(solution)/shard_map/spectral/pallas_call | solution.py:234
  63.9 4.6 %all-to-all-start.1 = ((bf16[128,32,128]{2,1,0:T(8,128)(2,1)}), bf16[128,32,128]{2,1,0:T(8,128)(2,1)S(1)}, u32[]{:S(2)}, u32[]{:S(2)}) async-start(bf16[128,32,128]{2,1,0:T(8,128)(2,1)} %spectral.1), calls=%async_computation.1 | async-start | bytes 2097152 | tf_op jit(solution)/shard_map/all_to_all | solution.py:307
  68.5 0.0 copy-done.11
  68.5 5.5 %fusion = (f32[128,4096]{1,0:T(8,128)S(1)}, f32[128,4096]{1,0:T(8,128)}) fusion(f32[130,4096]{1,0:T(8,128)} %maximum_convert_fusion, f32[4096]{0:T(1024)S(1)} %bitcast.4, f32[4096]{0:T(1024)S(1)} %bitcast.5, f32[4096]{0:T(1024)S(1)} %bitcast.3, bf16[128,4096]{1,0:T(8,128)(2,1)} %get-tuple-element.8, f32[4096]{0:T(1024)S(1)} %copy-done.11), kind=kLoop, calls=%fused_computation.1 | loop fusion | flops 3670016 | bytes 11599872 | tf_op jit(solution)/shard_map/add | solution.py:304
  74.0 13.9 %all-to-all-done.1.c_ref = bf16[128,32,128]{2,1,0:T(8,128)(2,1)S(1)} async-done(((bf16[128,32,128]{2,1,0:T(8,128)(2,1)}), bf16[128,32,128]{2,1,0:T(8,128)(2,1)S(1)}, u32[]{:S(2)}, u32[]{:S(2)}) %all-to-all-start.1) | async-done | bytes 1048608 | tf_op jit(solution)/shard_map/all_to_all | solution.py:307
  87.9 0.0 copy-start
  87.9 1.6 %copy-done = f32[128,4096]{1,0:T(8,128)S(1)} copy-done((f32[128,4096]{1,0:T(8,128)S(1)}, f32[128,4096]{1,0:T(8,128)}, u32[]{:S(2)}) %copy-start) | copy-done | bytes 2097176
  89.5 1.5 %mix.1 = bf16[128,4096]{1,0:T(8,128)(2,1)} custom-call(bf16[128,32,128]{2,1,0:T(8,128)(2,1)S(1)} %all-to-all-done.1.c_ref, f32[128,4096]{1,0:T(8,128)S(1)} %get-tuple-element.12.q_ref, f32[128,4096]{1,0:T(8,128)S(1)} %copy-done), custom_call_target="tpu_custom_call" | custom-call | tf_op jit(solution)/shard_map/mix/pallas_call | solution.py:278
  (1 shorter events, 0.0 us)
Async XLA Ops:
  1.0 12.2 %collective-permute-start = (bf16[2,12288]{1,0:T(2,128)(2,1)S(1)}, bf16[2,12288]{1,0:T(2,128)(2,1)S(1)}, u32[]{:S(2)}, u32[]{:S(2)}) collective-permute-start(bf16[2,12288]{1,0:T(2,128)(2,1)S(1)} %slice.27), channel_id=1, source_target_pairs={{0,1},{1,2},{2,3},{3,4},{4,5},{5,6},{6,7},{7,8},{8,9},{9,10},{10,1... | collective-permute-start | bytes 147464 | tf_op jit(solution)/shard_map/ppermute | solution.py:295
  13.2 0.6 copy-start.10
  21.0 6.2 %copy-start.9 = (bf16[3,12288]{1,0:T(4,128)(2,1)S(1)}, bf16[3,12288]{1,0:T(4,128)(2,1)}, u32[]{:S(2)}) copy-start(bf16[3,12288]{1,0:T(4,128)(2,1)} %wv_ref.1) | copy-start | bytes 221188
  21.0 36.7 %all-to-all-start = ((bf16[128,64,128]{2,1,0:T(8,128)(2,1)}), bf16[128,64,128]{2,1,0:T(8,128)(2,1)S(1)}, u32[]{:S(2)}, u32[]{:S(2)}) async-start(bf16[128,64,128]{2,1,0:T(8,128)(2,1)} %get-tuple-element.7), calls=%async_computation | async-start | bytes 4194304 | tf_op jit(solution)/shard_map/all_to_all | solution.py:299
  27.2 1.2 %slice-start = ((bf16[128,12288]{1,0:T(8,128)(2,1)}), bf16[128,4096]{1,0:T(8,128)(2,1)S(1)}, s32[]{:S(2)}) async-start(bf16[128,12288]{1,0:T(8,128)(2,1)} %v_ref.1), calls=%async_computation.2 | async-start | bytes 2097152 | tf_op jit(solution)/shard_map/slice | solution.py:300
  27.2 1.2 %slice-start.1 = ((bf16[2,12288]{1,0:T(2,128)(2,1)}), bf16[2,4096]{1,0:T(2,128)(2,1)S(1)}, s32[]{:S(2)}) async-start(bf16[2,12288]{1,0:T(2,128)(2,1)} %copy-done.10), calls=%async_computation.3 | async-start | bytes 32768 | tf_op jit(solution)/shard_map/slice | solution.py:300
  27.2 30.5 %copy-start.1 = (bf16[256,256]{1,0:T(8,128)(2,1)S(1)}, bf16[256,256]{1,0:T(8,128)(2,1)}, u32[]{:S(2)}) copy-start(bf16[256,256]{1,0:T(8,128)(2,1)} %constant.18.clone.bwd_ref) | copy-start | bytes 393220
  27.2 30.4 %copy-start.2 = (bf16[256,256]{1,0:T(8,128)(2,1)S(1)}, bf16[256,256]{1,0:T(8,128)(2,1)}, u32[]{:S(2)}) copy-start(bf16[256,256]{1,0:T(8,128)(2,1)} %constant.17.clone.fwd_ref) | copy-start | bytes 393220
  27.3 30.4 %copy-start.3 = (f32[128,128]{1,0:T(8,128)S(1)}, f32[128,128]{1,0:T(8,128)}, u32[]{:S(2)}) copy-start(f32[128,128]{1,0:T(8,128)} %constant.21.clone.ts_ref) | copy-start | bytes 196612
  27.3 30.4 %copy-start.4 = (f32[128,128]{1,0:T(8,128)S(1)}, f32[128,128]{1,0:T(8,128)}, u32[]{:S(2)}) copy-start(f32[128,128]{1,0:T(8,128)} %constant.20.clone.tc_ref) | copy-start | bytes 196612
  27.3 30.4 %copy-start.5 = (bf16[128,256]{1,0:T(8,128)(2,1)S(1)}, bf16[128,256]{1,0:T(8,128)(2,1)}, u32[]{:S(2)}) copy-start(bf16[128,256]{1,0:T(8,128)(2,1)} %constant.19.clone.last_ref) | copy-start | bytes 196612
  27.3 30.4 %copy-start.6 = (bf16[256,128]{1,0:T(8,128)(2,1)S(1)}, bf16[256,128]{1,0:T(8,128)(2,1)}, u32[]{:S(2)}) copy-start(bf16[256,128]{1,0:T(8,128)(2,1)} %constant.16.clone.first_ref) | copy-start | bytes 196612
  27.3 30.4 %copy-start.7 = (f32[1,128]{1,0:T(1,128)S(1)}, f32[1,128]{1,0:T(1,128)}, u32[]{:S(2)}) copy-start(f32[1,128]{1,0:T(1,128)} %constant.23.clone.hs_ref) | copy-start | bytes 1540
  27.3 30.4 %copy-start.8 = (f32[1,128]{1,0:T(1,128)S(1)}, f32[1,128]{1,0:T(1,128)}, u32[]{:S(2)}) copy-start(f32[1,128]{1,0:T(1,128)} %constant.22.clone.hc_ref) | copy-start | bytes 1540
  30.1 38.4 %copy-start.11 = (f32[4096]{0:T(1024)S(1)}, f32[4096]{0:T(1024)}, u32[]{:S(2)}) copy-start(f32[4096]{0:T(1024)} %param.15) | copy-start | bytes 49156
  63.9 24.0 %all-to-all-start.1 = ((bf16[128,32,128]{2,1,0:T(8,128)(2,1)}), bf16[128,32,128]{2,1,0:T(8,128)(2,1)S(1)}, u32[]{:S(2)}, u32[]{:S(2)}) async-start(bf16[128,32,128]{2,1,0:T(8,128)(2,1)} %spectral.1), calls=%async_computation.1 | async-start | bytes 2097152 | tf_op jit(solution)/shard_map/all_to_all | solution.py:307
  87.9 1.6 %copy-start = (f32[128,4096]{1,0:T(8,128)S(1)}, f32[128,4096]{1,0:T(8,128)}, u32[]{:S(2)}) copy-start(f32[128,4096]{1,0:T(8,128)} %get-tuple-element.13.s_ref) | copy-start | bytes 6291460

commit v3 on v1

--- a/solution.py
+++ b/solution.py
@@ -8,6 +8,7 @@
 from jax.experimental import pallas as pl
 from jax.experimental.pallas import tpu as pltpu
 from jax.sharding import PartitionSpec as P
+
 
 AXES = ("outer", "inner")
 F32 = jnp.float32
@@ -55,61 +56,112 @@
     )
 
 
-def featurized(rows, rim, taps):
-    rows = rows.astype(F32)
-    rim = rim.astype(F32)
-    taps = taps.astype(F32)
-    index = lax.broadcasted_iota(jnp.int32, rows.shape, 0)
-    back1 = jnp.where(index == 0, rim[1:2], pltpu.roll(rows, 1, 0))
-    back2 = pltpu.roll(rows, 2, 0)
-    back2 = jnp.where(index == 0, rim[0:1], jnp.where(index == 1, rim[1:2], back2))
-    return taps[0:1] * rows + taps[1:2] * back1 + taps[2:3] * back2
-
-
-def gate_kernel(k_ref, v_ref, rk_ref, rv_ref, wk_ref, wv_ref, f_ref, send_ref, gated_ref):
-    gated = featurized(k_ref[...], rk_ref[...], wk_ref[...]) * featurized(
-        v_ref[...], rv_ref[...], wv_ref[...]
-    )
-    gated = gated.astype(BF16)
-    gated_ref[...] = gated
-    dests, twice, tok = send_ref.shape
-    own = twice // 2
-    send_ref[:, :own, :] = gated.T.reshape(dests, own, tok)
-    send_ref[:, own:, :] = f_ref[...].T.reshape(dests, own, tok)
-
-
-def gate(projected, rim, short_filter, long_filter, devices):
+EXTRA = 8
+
+
+def in_hbm(value):
+    return pltpu.with_memory_space_constraint(value, pltpu.HBM)
+
+
+def gate_kernel(p_ref, f_ref, t_ref, send_ref, w_ref, k_buf, v_buf, f_buf, out_buf, k_ext, v_ext, e_ext, sem, tap_sem):
+    tok, width = f_ref.shape
+    devices, _, _ = send_ref.shape
+    own = width // devices
+    steps = sem.shape[0]
+    cols = width // steps
+    peers = devices // steps
+
+    def reads(i):
+        at = pl.ds(i * cols, cols)
+        return (
+            pltpu.make_async_copy(
+                p_ref.at[:, pl.ds(width + i * cols, cols)], k_buf.at[:, at], sem.at[i, 0]
+            ),
+            pltpu.make_async_copy(
+                p_ref.at[:, pl.ds(2 * width + i * cols, cols)], v_buf.at[:, at], sem.at[i, 1]
+            ),
+            pltpu.make_async_copy(f_ref.at[:, at], f_buf.at[:, at], sem.at[i, 2]),
+        )
+
+    def write(i):
+        at = pl.ds(i * peers, peers)
+        return pltpu.make_async_copy(out_buf.at[at], send_ref.at[at], sem.at[i, 3])
+
+    taps_read = pltpu.make_async_copy(t_ref, w_ref, tap_sem)
+    taps_read.start()
+    for i in range(steps):
+        for copy in reads(i):
+            copy.start()
+    lead = 8
+    lanes = k_ext.shape[2]
+    for j in range(cols // lanes):
+        k_ext[j, :lead] = jnp.zeros((lead, lanes), F32)
+        v_ext[j, :lead] = jnp.zeros((lead, lanes), F32)
+    taps_read.wait()
+    for i in range(steps):
+        for copy in reads(i):
+            copy.wait()
+        for j in range(cols // lanes):
+            start = i * cols + j * lanes
+            at = slice(start, start + lanes)
+
+            def featurized(buf, ext, base):
+                taps = w_ref[:, base + start : base + start + lanes].astype(F32)
+                ext[j, lead:] = buf[:, at].astype(F32)
+                return (
+                    taps[0:1] * ext[j, lead : lead + tok]
+                    + taps[1:2] * ext[j, pl.ds(lead - 1, tok)]
+                    + taps[2:3] * ext[j, pl.ds(lead - 2, tok)]
+                )
+
+            gated = featurized(k_buf, k_ext, width) * featurized(v_buf, v_ext, 2 * width)
+            near = lanes // own
+            to = slice(start // own, start // own + near)
+            out_buf[to, :own] = gated.astype(BF16).T.reshape(near, own, tok)
+            out_buf[to, own : 2 * own] = f_buf[:, at].T.reshape(near, own, tok)
+            e_ext[0:2] = k_ext[j, lead : lead + 2]
+            e_ext[2:4] = v_ext[j, lead : lead + 2]
+            e_ext[4:6] = k_ext[j, lead + tok - 2 : lead + tok]
+            e_ext[6:8] = v_ext[j, lead + tok - 2 : lead + tok]
+            tile = e_ext[...]
+            for k in range(near):
+                turned = pltpu.roll(tile, lanes - k * own, 1) if k else tile
+                out_buf[start // own + k, 2 * own :] = turned.astype(BF16)
+        write(i).start()
+    for i in range(steps):
+        write(i).wait()
+
+
+def gate(projected, short_filter, long_filter, devices):
     tok, width = long_filter.shape
     own = width // devices
     steps = 8
     cols = width // steps
-    peers = devices // steps
-
-    def col(third):
-        return lambda i: (0, i + third * steps)
-
+    rows = 2 * own + EXTRA
     return pl.pallas_call(
         gate_kernel,
-        grid=(steps,),
         in_specs=[
-            pl.BlockSpec((tok, cols), col(1)),
-            pl.BlockSpec((tok, cols), col(2)),
-            pl.BlockSpec((rim.shape[0], cols), col(1)),
-            pl.BlockSpec((rim.shape[0], cols), col(2)),
-            pl.BlockSpec((short_filter.shape[0], cols), col(1)),
-            pl.BlockSpec((short_filter.shape[0], cols), col(2)),
-            pl.BlockSpec((tok, cols), lambda i: (0, i)),
-        ],
-        out_specs=[
-            pl.BlockSpec((peers, 2 * own, tok), lambda i: (i, 0, 0)),
-            pl.BlockSpec((tok, cols), lambda i: (0, i)),
-        ],
-        out_shape=[
-            jax.ShapeDtypeStruct((devices, 2 * own, tok), BF16),
-            jax.ShapeDtypeStruct((tok, width), BF16),
-        ],
+            pl.BlockSpec(memory_space=pltpu.HBM),
+            pl.BlockSpec(memory_space=pltpu.HBM),
+            pl.BlockSpec(memory_space=pltpu.HBM),
+        ],
+        out_specs=pl.BlockSpec(memory_space=pltpu.HBM),
+        out_shape=pltpu.HBM((devices, rows, tok), BF16),
+        scratch_shapes=[
+            pltpu.VMEM(short_filter.shape, BF16),
+            pltpu.VMEM((tok, width), BF16),
+            pltpu.VMEM((tok, width), BF16),
+            pltpu.VMEM((tok, width), BF16),
+            pltpu.VMEM((devices, rows, tok), BF16),
+            pltpu.VMEM((cols // 128, tok + 8, 128), F32),
+            pltpu.VMEM((cols // 128, tok + 8, 128), F32),
+            pltpu.VMEM((EXTRA, 128), F32),
+            pltpu.SemaphoreType.DMA((steps, 4)),
+            pltpu.SemaphoreType.DMA(()),
+        ],
+        compiler_params=pltpu.CompilerParams(vmem_limit_bytes=16 << 20),
         name="gate",
-    )(projected, projected, rim, rim, short_filter, short_filter, long_filter)
+    )(in_hbm(projected), in_hbm(long_filter), in_hbm(short_filter))
 
 
 def dot(a, b):
@@ -117,22 +169,45 @@
 
 
 def spectral_kernel(
-    z_ref, first_ref, fwd_ref, bwd_ref, last_ref, tc_ref, ts_ref, hc_ref, hs_ref, out_ref,
-    rows_ref, spec_ref, half_ref, half_out_ref, prod_ref, back_ref, conv_ref,
+    z_ref, taps_ref, first_ref, fwd_ref, bwd_ref, last_ref, tc_ref, ts_ref, hc_ref, hs_ref,
+    out_ref, rows_ref, fix_ref, spec_ref, half_ref, half_out_ref, prod_ref, back_ref, conv_ref, block_ref, sem,
 ):
-    segments, both, tok = z_ref.shape
+    segments, rows, tok = z_ref.shape
+    both = rows - EXTRA
     own = both // 2
-    pitch = rows_ref.shape[0] // segments
+    pitch = rows_ref.shape[0] // (segments + 1)
     out_pitch = conv_ref.shape[0] // segments
     piece = 16
 
     def widen(i, carry):
         for j in range(piece):
             b = i * piece + j
-            rows_ref[pl.ds(b * pitch, both), :] = z_ref[b].astype(F32)
+            rows_ref[pl.ds((b + 1) * pitch, rows), :] = z_ref[b].astype(F32)
         return carry
 
     lax.fori_loop(0, segments // piece, widen, 0)
+
+    rows_ref[both:rows, :] = jnp.zeros((EXTRA, tok), F32)
+
+    def sent(row, before):
+        return rows_ref[pl.ds(both + row + (1 - before) * pitch, segments, stride=pitch), :]
+
+    def edge(tap, at):
+        now0, now1 = sent(at, 0), sent(at + 1, 0)
+        ago2, ago1 = sent(at + 4, 1), sent(at + 5, 1)
+        taps = [taps_ref[tap + n : tap + n + 1, :] for n in range(3)]
+        return (
+            taps[0] * now0 + taps[1] * ago1 + taps[2] * ago2,
+            taps[0] * now1 + taps[1] * now0 + taps[2] * ago1,
+        )
+
+    key0, key1 = edge(0, 0)
+    value0, value1 = edge(3, 2)
+    gated0 = key0 * value0
+    gated1 = pltpu.roll(key1 * value1, 1, 1)
+    lane = lax.broadcasted_iota(jnp.int32, (segments, tok), 1)
+    fix_ref[0] = jnp.where(lane % 2 == 0, gated0, gated1)
+    fix_ref[1] = jnp.where(lane % 2 == 1, gated0, gated1)
 
     top = 8
     index = lax.broadcasted_iota(jnp.int32, (top, tok), 0)
@@ -147,10 +222,13 @@
     def first_section(which, i, carry):
         start = i * group
         base = which * own + start
-        cols = [
-            rows_ref[pl.ds(base + j, segments, stride=pitch), :].astype(BF16)
-            for j in range(group)
-        ]
+        cols = []
+        for j in range(group):
+            col = rows_ref[pl.ds(base + j + pitch, segments, stride=pitch), :]
+            if which == 0:
+                fixed = pltpu.roll(fix_ref[j % 2], (tok - start - j) % tok, 1)
+                col = jnp.where(lane < 2, fixed, col)
+            cols.append(col.astype(BF16))
         out = dot(first_ref[...], jnp.concatenate(cols, 1))
         out = out.reshape(segments // top, 2, top, group * tok)
         tc, ts = tc_ref[...], ts_ref[...]
@@ -219,78 +297,164 @@
 
     lax.fori_loop(0, own // group4, finish, 0)
 
-    def narrow(i, carry):
-        for j in range(piece):
-            b = i * piece + j
-            out_ref[b] = conv_ref[pl.ds(b * out_pitch, own), :].astype(BF16)
-        return carry
-
-    lax.fori_loop(0, segments // piece, narrow, 0)
-
-
-def spectral(received, consts):
-    segments, both, tok = received.shape
+    def write(i):
+        at = pl.ds(i * piece, piece)
+        return pltpu.make_async_copy(block_ref.at[at], out_ref.at[at], sem.at[i])
+
+    for i in range(segments // piece):
+        for b in range(i * piece, (i + 1) * piece):
+            block_ref[b] = conv_ref[b * out_pitch : b * out_pitch + own, :].astype(BF16)
+        write(i).start()
+    for i in range(segments // piece):
+        write(i).wait()
+
+
+def spectral(received, taps, consts):
+    segments, rows, tok = received.shape
+    both = rows - EXTRA
     own = both // 2
     return pl.pallas_call(
         spectral_kernel,
-        out_shape=jax.ShapeDtypeStruct((segments, own, tok), BF16),
-        in_specs=[pl.BlockSpec(memory_space=pltpu.VMEM)] * 9,
-        out_specs=pl.BlockSpec(memory_space=pltpu.VMEM),
+        out_shape=pltpu.HBM((segments, own, tok), BF16),
+        in_specs=[pl.BlockSpec(memory_space=pltpu.VMEM)] * 10,
+        out_specs=pl.BlockSpec(memory_space=pltpu.HBM),
         scratch_shapes=[
-            pltpu.VMEM((segments * (both + PAD), tok), F32),
+            pltpu.VMEM(((segments + 1) * (rows + PAD), tok), F32),
+            pltpu.VMEM((2, segments, tok), F32),
             pltpu.VMEM((own, segments // 16, 2, 16, 2 * tok), BF16),
             pltpu.VMEM((both, tok), F32),
             pltpu.VMEM((own, tok), F32),
             pltpu.VMEM((own, segments, 2 * tok), BF16),
             pltpu.VMEM((own, 2 * segments, tok), BF16),
             pltpu.VMEM((segments * (own + PAD), tok), F32),
-        ],
+            pltpu.VMEM((segments, own, tok), BF16),
+            pltpu.SemaphoreType.DMA((segments // 16,)),
+        ],
+        compiler_params=pltpu.CompilerParams(vmem_limit_bytes=28 << 20),
         name="spectral",
-    )(received, *consts)
-
-
-def mix_kernel(c_ref, q_ref, s_ref, out_ref):
+    )(resident(received), taps, *consts)
+
+
+def mix_kernel(c_ref, q_ref, skip_ref, g_ref, out_ref, g_buf, buf_ref, sem):
     peers, own, tok = c_ref.shape
-    conv = c_ref[...].reshape(peers * own, tok).T.astype(F32)
-    out_ref[...] = (q_ref[...] * (conv + s_ref[...])).astype(BF16)
-
-
-def mix(conv, query, direct):
+    steps = sem.shape[0]
+    peers = peers // steps
+    cols = peers * own
+
+    def read(i):
+        at = pl.ds(i * cols, cols)
+        return pltpu.make_async_copy(g_ref.at[:, at], g_buf.at[:, at], sem.at[i, 0])
+
+    def write(i):
+        at = pl.ds(i * cols, cols)
+        return pltpu.make_async_copy(buf_ref.at[:, at], out_ref.at[:, at], sem.at[i, 1])
+
+    for i in range(steps):
+        read(i).start()
+    for i in range(steps):
+        at = slice(i * cols, (i + 1) * cols)
+        conv = c_ref[i * peers : (i + 1) * peers].reshape(cols, tok).T.astype(F32)
+        read(i).wait()
+        direct = skip_ref[:, at] * g_buf[:, at].astype(F32)
+        buf_ref[:, at] = (q_ref[:, at] * (conv + direct)).astype(BF16)
+        write(i).start()
+    for i in range(steps):
+        write(i).wait()
+
+
+def resident(value):
+    return pltpu.with_memory_space_constraint(value, pltpu.VMEM)
+
+
+def mix(conv, query, skip, gated):
     devices, own, tok = conv.shape
     width = devices * own
     steps = 8
+    return pl.pallas_call(
+        mix_kernel,
+        in_specs=[pl.BlockSpec(memory_space=pltpu.VMEM)] * 3
+        + [pl.BlockSpec(memory_space=pltpu.HBM)],
+        out_specs=pl.BlockSpec(memory_space=pltpu.HBM),
+        out_shape=jax.ShapeDtypeStruct((tok, width), BF16),
+        scratch_shapes=[
+            pltpu.VMEM((tok, width), BF16),
+            pltpu.VMEM((tok, width), BF16),
+            pltpu.SemaphoreType.DMA((steps, 2)),
+        ],
+        compiler_params=pltpu.CompilerParams(vmem_limit_bytes=6 << 20),
+        name="mix",
+    )(resident(conv), resident(query), resident(skip), in_hbm(gated))
+
+
+def side_kernel(q_ref, k_ref, v_ref, rq_ref, rk_ref, rv_ref, wq_ref, wk_ref, wv_ref,
+                query_ref, gated_ref):
+    def featurized(rows_ref, rim_ref, taps_ref):
+        rows = rows_ref[...].astype(F32)
+        rim = rim_ref[...].astype(F32)
+        taps = taps_ref[...].astype(F32)
+        index = lax.broadcasted_iota(jnp.int32, rows.shape, 0)
+        back1 = jnp.where(index == 0, rim[1:2], pltpu.roll(rows, 1, 0))
+        back2 = pltpu.roll(rows, 2, 0)
+        back2 = jnp.where(index == 0, rim[0:1], jnp.where(index == 1, rim[1:2], back2))
+        return taps[0:1] * rows + taps[1:2] * back1 + taps[2:3] * back2
+
+    query_ref[...] = featurized(q_ref, rq_ref, wq_ref)
+    gated = featurized(k_ref, rk_ref, wk_ref) * featurized(v_ref, rv_ref, wv_ref)
+    gated_ref[...] = gated.astype(BF16)
+
+
+def side(projected, rim, short_filter):
+    tok = projected.shape[0]
+    width = projected.shape[1] // 3
+    steps = 8
     cols = width // steps
+
+    def thirds(rows):
+        return [
+            pl.BlockSpec((rows, cols), functools.partial(lambda third, i: (0, i + third * steps), t))
+            for t in range(3)
+        ]
+
     wide = pl.BlockSpec((tok, cols), lambda i: (0, i))
     return pl.pallas_call(
-        mix_kernel,
+        side_kernel,
         grid=(steps,),
-        in_specs=[pl.BlockSpec((devices // steps, own, tok), lambda i: (i, 0, 0)), wide, wide],
-        out_specs=wide,
-        out_shape=jax.ShapeDtypeStruct((tok, width), BF16),
-        name="mix",
-    )(conv, query, direct)
+        in_specs=thirds(tok)
+        + thirds(rim.shape[0])
+        + thirds(short_filter.shape[0]),
+        out_specs=[wide, wide],
+        out_shape=[
+            jax.ShapeDtypeStruct((tok, width), F32),
+            pltpu.HBM((tok, width), BF16),
+        ],
+        compiler_params=pltpu.CompilerParams(vmem_limit_bytes=8 << 20),
+        name="side",
+    )(*[in_hbm(projected)] * 3, *[rim] * 3, *[short_filter] * 3)
 
 
 def shards(projected, short_filter, long_filter, skip):
     devices = lax.axis_size(AXES)
     tok, width = long_filter.shape
+    own = width // devices
     tap_count = short_filter.shape[0]
     rim_count = tap_count - 1
     consts = tables(devices, tok)
-    rim = lax.ppermute(
-        projected[tok - rim_count :], AXES, [(i, i + 1) for i in range(devices - 1)]
-    )
-    send, gated = gate(projected, rim, short_filter, long_filter, devices)
+    position = lax.axis_index(AXES)
+    taps = jnp.concatenate(
+        [
+            lax.dynamic_slice_in_dim(short_filter, third * width + position * own, own, 1)
+            for third in (1, 2)
+        ],
+        0,
+    ).astype(F32)
+    taps = jnp.pad(taps, ((0, 8 - 2 * tap_count), (0, tok - own)))
+    send = gate(projected, short_filter, long_filter, devices)
     received = lax.all_to_all(send, AXES, split_axis=0, concat_axis=0, tiled=True)
-    extended = jnp.concatenate([rim[:, :width], projected[:, :width]], 0).astype(F32)
-    query = jnp.zeros((tok, width), F32)
-    for tap in range(tap_count):
-        offset = rim_count - tap
-        query = query + short_filter[tap, :width].astype(F32) * extended[offset : offset + tok]
-    direct = skip[None, :] * gated.astype(F32)
-    conv = spectral(received, consts)
+    rim = lax.ppermute(projected[tok - rim_count :], AXES, [(i, i + 1) for i in range(devices - 1)])
+    query, gated = side(projected, rim, short_filter)
+    conv = spectral(received, taps, consts)
     conv = lax.all_to_all(conv, AXES, split_axis=0, concat_axis=0, tiled=True)
-    return mix(conv, query, direct)
+    return mix(conv, query, skip[None, :], gated)
 
 
 def solution(mesh):

time: 97.6 us -> 89.9 us (0.921)
  waiting for transfers between devices: 52.3 us -> 47.9 us
  other arithmetic: 4.26 us -> 0.01 us
  starting transfers between devices: 15.2 us -> 19.4 us
  local copies, waits for them, and re-layouts: 3.73 us -> 1.13 us
    all_to_all x1, waiting for transfers between devices: 15.4 us -> 0.01 us  [shards(): conv = lax.all_to_all(conv, AXES, split_axis=0, concat_axis=0, tiled=True)]
    ppermute x1, waiting for transfers between devices: 8.24 us -> 14.7 us  [shards(): lax.ppermute(projected[tok - rim_count:], AXES, [(i, i + 1) for i in rang...]
    all_to_all x1, starting transfers between devices: 6.64 us -> 11.5 us  [shards(): lax.all_to_all(send, AXES, split_axis=0, concat_axis=0, tiled=True)]
    all_to_all x1, waiting for transfers between devices: 28.6 us -> 33.2 us  [shards(): lax.all_to_all(send, AXES, split_axis=0, concat_axis=0, tiled=True)]
    add x1 -> x0, other arithmetic: 3.93 us -> none  [shards(): query + short_filter[tap, :width].astype(F32) * extended[offset:offset +...]
    unnamed x8 -> x20, local copies, waits for them, and re-layouts: 1.59 us -> 0.07 us
    slice x4 -> x0, local copies, waits for them, and re-layouts: 1.16 us -> none  [the longest x2 1.16 us: shards(): projected[:, :width]]
    pallas_call x3 -> x4, Pallas kernels: 21.4 us -> 20.8 us  [the longest x1 6.99 us: side(): pl.pallas_call(side_kernel, grid=(steps,), in_specs=thirds(tok) + thirds(...]
  transfers between devices with their start and end apart: 3 -> 3, of which waited for: 3 -> 2; matrix products, arithmetic and copies ran while one was open for 4% -> 1% of each run, Pallas kernels for 0% -> 8%
where the time goes in v3:
time: 89.9 us; the launch traced here: 89.4 us
  waiting for transfers between devices  47.9 us (53%)
  Pallas kernels  20.8 us (23%)
  starting transfers between devices  19.4 us (22%)
  local copies, waits for them, and re-layouts  1.13 us (1%)
    all_to_all x1, waiting for transfers between devices, shards(): lax.all_to_all(send, AXES, split_axis=0, concat_axis=0, tiled=True)  33.2 us
    ppermute x1, waiting for transfers between devices, shards(): lax.ppermute(projected[tok - rim_count:], AXES, [(i, i + 1) for i in rang...  14.7 us
    all_to_all x1, starting transfers between devices, shards(): lax.all_to_all(send, AXES, split_axis=0, concat_axis=0, tiled=True)  11.5 us
    pallas_call x1, Pallas kernels, side(): pl.pallas_call(side_kernel, grid=(steps,), in_specs=thirds(tok) + thirds(...  6.99 us
    pallas_call x1, Pallas kernels, spectral(): pl.pallas_call(spectral_kernel, out_shape=pltpu.HBM((segments, own, tok),...  6.45 us
    pallas_call x1, Pallas kernels, gate(): pl.pallas_call(gate_kernel, in_specs=[pl.BlockSpec(memory_space=pltpu.HBM...  4.86 us
    all_to_all x1, starting transfers between devices, shards(): conv = lax.all_to_all(conv, AXES, split_axis=0, concat_axis=0, tiled=True)  4.61 us
    ppermute x1, starting transfers between devices, shards(): lax.ppermute(projected[tok - rim_count:], AXES, [(i, i + 1) for i in rang...  3.28 us
  transfers between devices with their start and end apart: 3, of which 2 were waited for; matrix products, arithmetic and copies ran while one was open for 1% of the time, Pallas kernels for 8%

profile of v3, /device:TPU:1, one launch (start us, length us, event | category | flops | bytes accessed | tf_op | source)
XLA Modules:
  0.0 89.4 jit_solution(16910577061847965708)
XLA Ops:
  0.0 4.9 %gate.1 = bf16[128,72,128]{2,1,0:T(8,128)(2,1)} custom-call(bf16[128,12288]{1,0:T(8,128)(2,1)} %v_ref.1, bf16[128,4096]{1,0:T(8,128)(2,1)} %f_ref.1, bf16[3,12288]{1,0:T(4,128)(2,1)} %wv_ref.1), custom_call_target="tpu_custom_call" | custom-call | tf_op jit(solution)/shard_map/gate/pallas_call | solution.py:141
  4.9 0.0 copy-start
  4.9 0.0 copy-start.1
  4.9 0.0 copy-start.2
  4.9 0.0 copy-start.3
  4.9 0.0 copy-start.4
  4.9 0.0 copy-start.5
  4.9 0.0 copy-start.6
  5.0 0.0 copy-start.8
  5.0 0.0 copy-start.9
  5.0 11.5 %all-to-all-start = ((bf16[128,72,128]{2,1,0:T(8,128)(2,1)}), bf16[128,72,128]{2,1,0:T(8,128)(2,1)S(1)}, u32[]{:S(2)}, u32[]{:S(2)}) async-start(bf16[128,72,128]{2,1,0:T(8,128)(2,1)} %gate.1), calls=%async_computation | async-start | bytes 4718592 | tf_op jit(solution)/shard_map/all_to_all | solution.py:452
  16.5 0.0 copy-done
  16.5 0.1 constant_dynamic-slice_fusion.1
  16.6 33.2 %all-to-all-done.z_ref = bf16[128,72,128]{2,1,0:T(8,128)(2,1)S(1)} async-done(((bf16[128,72,128]{2,1,0:T(8,128)(2,1)}), bf16[128,72,128]{2,1,0:T(8,128)(2,1)S(1)}, u32[]{:S(2)}, u32[]{:S(2)}) %all-to-all-start) | async-done | bytes 2359328 | tf_op jit(solution)/shard_map/all_to_all | solution.py:452
  49.8 0.0 copy-done.1
  49.8 0.0 copy-done.2
  49.8 0.0 copy-done.3
  49.8 0.0 copy-done.4
  49.8 0.0 copy-done.5
  49.8 0.0 copy-done.6
  49.8 0.0 copy-done.8
  49.8 0.0 copy-done.9
  49.8 6.5 %spectral.1 = bf16[128,32,128]{2,1,0:T(8,128)(2,1)} custom-call(bf16[128,72,128]{2,1,0:T(8,128)(2,1)S(1)} %all-to-all-done.z_ref, f32[8,128]{1,0:T(8,128)S(1)} %fusion.6.taps_ref, bf16[256,128]{1,0:T(8,128)(2,1)S(1)} %copy-done.6, bf16[256,256]{1,0:T(8,128)(2,1)S(1)} %copy-done.2, bf16[256,256]{1,0:T(8,128)(2,1)S(1)} %copy-done.1, ...), custom_call_target="tpu_custom_call" | custom-call | tf_op jit(solution)/shard_map/spectral/pallas_call | solution.py:316
  56.3 4.6 %all-to-all-start.1 = ((bf16[128,32,128]{2,1,0:T(8,128)(2,1)}), bf16[128,32,128]{2,1,0:T(8,128)(2,1)S(1)}, u32[]{:S(2)}, u32[]{:S(2)}) async-start(bf16[128,32,128]{2,1,0:T(8,128)(2,1)} %spectral.1), calls=%async_computation.1 | async-start | bytes 2097152 | tf_op jit(solution)/shard_map/all_to_all | solution.py:456
  60.9 1.0 %slice.3 = bf16[2,12288]{1,0:T(2,128)(2,1)S(1)} slice(bf16[128,12288]{1,0:T(8,128)(2,1)} %v_ref.1), slice={[126:128], [0:12288]} | slice | bytes 98304 | tf_op jit(solution)/shard_map/slice | solution.py:453
  61.9 0.0 copy-start.7
  61.9 3.3 %collective-permute-start = (bf16[2,12288]{1,0:T(2,128)(2,1)S(1)}, bf16[2,12288]{1,0:T(2,128)(2,1)S(1)}, u32[]{:S(2)}, u32[]{:S(2)}) collective-permute-start(bf16[2,12288]{1,0:T(2,128)(2,1)S(1)} %slice.3), channel_id=1, source_target_pairs={{0,1},{1,2},{2,3},{3,4},{4,5},{5,6},{6,7},{7,8},{8,9},{9,10},{10,1... | collective-permute-start | bytes 147464 | tf_op jit(solution)/shard_map/ppermute | solution.py:453
  65.2 14.7 %collective-permute-done.rq_ref.rk_ref.rv_ref = bf16[2,12288]{1,0:T(2,128)(2,1)S(1)} collective-permute-done((bf16[2,12288]{1,0:T(2,128)(2,1)S(1)}, bf16[2,12288]{1,0:T(2,128)(2,1)S(1)}, u32[]{:S(2)}, u32[]{:S(2)}) %collective-permute-start) | collective-permute-done | bytes 49184 | tf_op jit(solution)/shard_map/ppermute | solution.py:453
  79.9 7.0 %side.1 = (f32[128,4096]{1,0:T(8,128)S(1)}, bf16[128,4096]{1,0:T(8,128)(2,1)}) custom-call(bf16[128,12288]{1,0:T(8,128)(2,1)} %v_ref.1, bf16[128,12288]{1,0:T(8,128)(2,1)} %v_ref.1, bf16[128,12288]{1,0:T(8,128)(2,1)} %v_ref.1, bf16[2,12288]{1,0:T(2,128)(2,1)S(1)} %collective-permute-done.rq_ref.rk_ref.rv_ref, ...), custom_call_target="tpu_custom_call" | custom-call | tf_op jit(solution)/shard_map/side/pallas_call | solution.py:419
  86.9 0.0 all-to-all-done.1.c_ref
  86.9 0.0 copy-done.7
  86.9 2.5 %mix.1 = bf16[128,4096]{1,0:T(8,128)(2,1)} custom-call(bf16[128,32,128]{2,1,0:T(8,128)(2,1)S(1)} %all-to-all-done.1.c_ref, f32[128,4096]{1,0:T(8,128)S(1)} %get-tuple-element.7.q_ref, f32[1,4096]{1,0:T(1,128)S(1)} %bitcast.1, bf16[128,4096]{1,0:T(8,128)(2,1)} %get-tuple-element.8.g_ref), custom_call_target="tpu_custom_call" | custom-call | tf_op jit(solution)/shard_map/mix/pallas_call | solution.py:373
  (1 shorter events, 0.0 us)
Async XLA Ops:
  4.9 11.6 %copy-start = (bf16[3,12288]{1,0:T(4,128)(2,1)S(1)}, bf16[3,12288]{1,0:T(4,128)(2,1)}, u32[]{:S(2)}) copy-start(bf16[3,12288]{1,0:T(4,128)(2,1)} %wv_ref.1) | copy-start | bytes 221188
  4.9 44.9 %copy-start.1 = (bf16[256,256]{1,0:T(8,128)(2,1)S(1)}, bf16[256,256]{1,0:T(8,128)(2,1)}, u32[]{:S(2)}) copy-start(bf16[256,256]{1,0:T(8,128)(2,1)} %constant.43.clone.bwd_ref) | copy-start | bytes 393220
  4.9 44.9 %copy-start.2 = (bf16[256,256]{1,0:T(8,128)(2,1)S(1)}, bf16[256,256]{1,0:T(8,128)(2,1)}, u32[]{:S(2)}) copy-start(bf16[256,256]{1,0:T(8,128)(2,1)} %constant.42.clone.fwd_ref) | copy-start | bytes 393220
  4.9 44.9 %copy-start.3 = (f32[128,128]{1,0:T(8,128)S(1)}, f32[128,128]{1,0:T(8,128)}, u32[]{:S(2)}) copy-start(f32[128,128]{1,0:T(8,128)} %constant.46.clone.ts_ref) | copy-start | bytes 196612
  4.9 44.9 %copy-start.4 = (f32[128,128]{1,0:T(8,128)S(1)}, f32[128,128]{1,0:T(8,128)}, u32[]{:S(2)}) copy-start(f32[128,128]{1,0:T(8,128)} %constant.45.clone.tc_ref) | copy-start | bytes 196612
  4.9 44.9 %copy-start.5 = (bf16[128,256]{1,0:T(8,128)(2,1)S(1)}, bf16[128,256]{1,0:T(8,128)(2,1)}, u32[]{:S(2)}) copy-start(bf16[128,256]{1,0:T(8,128)(2,1)} %constant.44.clone.last_ref) | copy-start | bytes 196612
  4.9 44.9 %copy-start.6 = (bf16[256,128]{1,0:T(8,128)(2,1)S(1)}, bf16[256,128]{1,0:T(8,128)(2,1)}, u32[]{:S(2)}) copy-start(bf16[256,128]{1,0:T(8,128)(2,1)} %constant.41.clone.first_ref) | copy-start | bytes 196612
  5.0 44.9 %copy-start.8 = (f32[1,128]{1,0:T(1,128)S(1)}, f32[1,128]{1,0:T(1,128)}, u32[]{:S(2)}) copy-start(f32[1,128]{1,0:T(1,128)} %constant.48.clone.hs_ref) | copy-start | bytes 1540
  5.0 44.9 %copy-start.9 = (f32[1,128]{1,0:T(1,128)S(1)}, f32[1,128]{1,0:T(1,128)}, u32[]{:S(2)}) copy-start(f32[1,128]{1,0:T(1,128)} %constant.47.clone.hc_ref) | copy-start | bytes 1540
  5.0 44.8 %all-to-all-start = ((bf16[128,72,128]{2,1,0:T(8,128)(2,1)}), bf16[128,72,128]{2,1,0:T(8,128)(2,1)S(1)}, u32[]{:S(2)}, u32[]{:S(2)}) async-start(bf16[128,72,128]{2,1,0:T(8,128)(2,1)} %gate.1), calls=%async_computation | async-start | bytes 4718592 | tf_op jit(solution)/shard_map/all_to_all | solution.py:452
  56.3 30.6 %all-to-all-start.1 = ((bf16[128,32,128]{2,1,0:T(8,128)(2,1)}), bf16[128,32,128]{2,1,0:T(8,128)(2,1)S(1)}, u32[]{:S(2)}, u32[]{:S(2)}) async-start(bf16[128,32,128]{2,1,0:T(8,128)(2,1)} %spectral.1), calls=%async_computation.1 | async-start | bytes 2097152 | tf_op jit(solution)/shard_map/all_to_all | solution.py:456
  61.9 25.0 %copy-start.7 = (f32[4096]{0:T(1024)S(1)}, f32[4096]{0:T(1024)}, u32[]{:S(2)}) copy-start(f32[4096]{0:T(1024)} %param.15) | copy-start | bytes 49156
  61.9 18.0 %collective-permute-start = (bf16[2,12288]{1,0:T(2,128)(2,1)S(1)}, bf16[2,12288]{1,0:T(2,128)(2,1)S(1)}, u32[]{:S(2)}, u32[]{:S(2)}) collective-permute-start(bf16[2,12288]{1,0:T(2,128)(2,1)S(1)} %slice.3), channel_id=1, source_target_pairs={{0,1},{1,2},{2,3},{3,4},{4,5},{5,6},{6,7},{7,8},{8,9},{9,10},{10,1... | collective-permute-start | bytes 147464 | tf_op jit(solution)/shard_map/ppermute | solution.py:453

commit v4 on v3

--- a/solution.py
+++ b/solution.py
@@ -340,6 +340,7 @@
     steps = sem.shape[0]
     peers = peers // steps
     cols = peers * own
+    near = 128 // own
 
     def read(i):
         at = pl.ds(i * cols, cols)
@@ -352,11 +353,12 @@
     for i in range(steps):
         read(i).start()
     for i in range(steps):
-        at = slice(i * cols, (i + 1) * cols)
-        conv = c_ref[i * peers : (i + 1) * peers].reshape(cols, tok).T.astype(F32)
         read(i).wait()
-        direct = skip_ref[:, at] * g_buf[:, at].astype(F32)
-        buf_ref[:, at] = (q_ref[:, at] * (conv + direct)).astype(BF16)
+        for j in range(i * peers, (i + 1) * peers, near):
+            at = slice(j * own, (j + near) * own)
+            conv = c_ref[j : j + near].reshape(near * own, tok).T.astype(F32)
+            direct = skip_ref[:, at] * g_buf[:, at].astype(F32)
+            buf_ref[:, at] = (q_ref[:, at] * (conv + direct)).astype(BF16)
         write(i).start()
     for i in range(steps):
         write(i).wait()
@@ -424,7 +426,7 @@
         + thirds(short_filter.shape[0]),
         out_specs=[wide, wide],
         out_shape=[
-            jax.ShapeDtypeStruct((tok, width), F32),
+            pltpu.HBM((tok, width), F32),
             pltpu.HBM((tok, width), BF16),
         ],
         compiler_params=pltpu.CompilerParams(vmem_limit_bytes=8 << 20),

time: 89.9 us -> 91.4 us (1.017)
  local copies, waits for them, and re-layouts: 1.13 us -> 2.71 us
    unnamed x20 -> x22, local copies, waits for them, and re-layouts: 0.07 us -> 1.65 us
where the time goes in v4:
time: 91.4 us; the launch traced here: 90.9 us
  waiting for transfers between devices  47.9 us (52%)
  Pallas kernels  20.8 us (23%)
  starting transfers between devices  19.4 us (21%)
  local copies, waits for them, and re-layouts  2.71 us (3%)
    all_to_all x1, waiting for transfers between devices, shards(): lax.all_to_all(send, AXES, split_axis=0, concat_axis=0, tiled=True)  33.2 us
    ppermute x1, waiting for transfers between devices, shards(): lax.ppermute(projected[tok - rim_count:], AXES, [(i, i + 1) for i in rang...  14.7 us
    all_to_all x1, starting transfers between devices, shards(): lax.all_to_all(send, AXES, split_axis=0, concat_axis=0, tiled=True)  11.5 us
    pallas_call x1, Pallas kernels, side(): pl.pallas_call(side_kernel, grid=(steps,), in_specs=thirds(tok) + thirds(...  7.03 us
    pallas_call x1, Pallas kernels, spectral(): pl.pallas_call(spectral_kernel, out_shape=pltpu.HBM((segments, own, tok),...  6.46 us
    pallas_call x1, Pallas kernels, gate(): pl.pallas_call(gate_kernel, in_specs=[pl.BlockSpec(memory_space=pltpu.HBM...  4.85 us
    all_to_all x1, starting transfers between devices, shards(): conv = lax.all_to_all(conv, AXES, split_axis=0, concat_axis=0, tiled=True)  4.6 us
    ppermute x1, starting transfers between devices, shards(): lax.ppermute(projected[tok - rim_count:], AXES, [(i, i + 1) for i in rang...  3.28 us
  transfers between devices with their start and end apart: 3, of which 2 were waited for; matrix products, arithmetic and copies ran while one was open for 1% of the time, Pallas kernels for 8%

profile of v4, /device:TPU:1, one launch (start us, length us, event | category | flops | bytes accessed | tf_op | source)
XLA Modules:
  0.0 90.9 jit_solution(14130458920211924332)
XLA Ops:
  0.0 4.9 %gate.1 = bf16[128,72,128]{2,1,0:T(8,128)(2,1)} custom-call(bf16[128,12288]{1,0:T(8,128)(2,1)} %v_ref.1, bf16[128,4096]{1,0:T(8,128)(2,1)} %f_ref.1, bf16[3,12288]{1,0:T(4,128)(2,1)} %wv_ref.1), custom_call_target="tpu_custom_call" | custom-call | tf_op jit(solution)/shard_map/gate/pallas_call | solution.py:141
  4.9 0.0 copy-start.1
  4.9 0.0 copy-start.2
  4.9 0.0 copy-start.3
  4.9 0.0 copy-start.4
  4.9 0.0 copy-start.5
  4.9 0.0 copy-start.6
  4.9 0.0 copy-start.7
  4.9 0.0 copy-start.9
  5.0 0.0 copy-start.10
  5.0 11.5 %all-to-all-start = ((bf16[128,72,128]{2,1,0:T(8,128)(2,1)}), bf16[128,72,128]{2,1,0:T(8,128)(2,1)S(1)}, u32[]{:S(2)}, u32[]{:S(2)}) async-start(bf16[128,72,128]{2,1,0:T(8,128)(2,1)} %gate.1), calls=%async_computation | async-start | bytes 4718592 | tf_op jit(solution)/shard_map/all_to_all | solution.py:454
  16.5 0.0 copy-done.1
  16.5 0.1 constant_dynamic-slice_fusion.1
  16.6 33.2 %all-to-all-done.z_ref = bf16[128,72,128]{2,1,0:T(8,128)(2,1)S(1)} async-done(((bf16[128,72,128]{2,1,0:T(8,128)(2,1)}), bf16[128,72,128]{2,1,0:T(8,128)(2,1)S(1)}, u32[]{:S(2)}, u32[]{:S(2)}) %all-to-all-start) | async-done | bytes 2359328 | tf_op jit(solution)/shard_map/all_to_all | solution.py:454
  49.8 0.0 copy-done.2
  49.8 0.0 copy-done.3
  49.8 0.0 copy-done.4
  49.8 0.0 copy-done.5
  49.8 0.0 copy-done.6
  49.8 0.0 copy-done.7
  49.8 0.0 copy-done.9
  49.8 0.0 copy-done.10
  49.8 6.5 %spectral.1 = bf16[128,32,128]{2,1,0:T(8,128)(2,1)} custom-call(bf16[128,72,128]{2,1,0:T(8,128)(2,1)S(1)} %all-to-all-done.z_ref, f32[8,128]{1,0:T(8,128)S(1)} %fusion.6.taps_ref, bf16[256,128]{1,0:T(8,128)(2,1)S(1)} %copy-done.7, bf16[256,256]{1,0:T(8,128)(2,1)S(1)} %copy-done.3, bf16[256,256]{1,0:T(8,128)(2,1)S(1)} %copy-done.2, ...), custom_call_target="tpu_custom_call" | custom-call | tf_op jit(solution)/shard_map/spectral/pallas_call | solution.py:316
  56.3 4.6 %all-to-all-start.1 = ((bf16[128,32,128]{2,1,0:T(8,128)(2,1)}), bf16[128,32,128]{2,1,0:T(8,128)(2,1)S(1)}, u32[]{:S(2)}, u32[]{:S(2)}) async-start(bf16[128,32,128]{2,1,0:T(8,128)(2,1)} %spectral.1), calls=%async_computation.1 | async-start | bytes 2097152 | tf_op jit(solution)/shard_map/all_to_all | solution.py:458
  60.9 1.0 %slice.3 = bf16[2,12288]{1,0:T(2,128)(2,1)S(1)} slice(bf16[128,12288]{1,0:T(8,128)(2,1)} %v_ref.1), slice={[126:128], [0:12288]} | slice | bytes 98304 | tf_op jit(solution)/shard_map/slice | solution.py:455
  61.9 0.0 copy-start.8
  61.9 3.3 %collective-permute-start = (bf16[2,12288]{1,0:T(2,128)(2,1)S(1)}, bf16[2,12288]{1,0:T(2,128)(2,1)S(1)}, u32[]{:S(2)}, u32[]{:S(2)}) collective-permute-start(bf16[2,12288]{1,0:T(2,128)(2,1)S(1)} %slice.3), channel_id=1, source_target_pairs={{0,1},{1,2},{2,3},{3,4},{4,5},{5,6},{6,7},{7,8},{8,9},{9,10},{10,1... | collective-permute-start | bytes 147464 | tf_op jit(solution)/shard_map/ppermute | solution.py:455
  65.2 14.7 %collective-permute-done.rq_ref.rk_ref.rv_ref = bf16[2,12288]{1,0:T(2,128)(2,1)S(1)} collective-permute-done((bf16[2,12288]{1,0:T(2,128)(2,1)S(1)}, bf16[2,12288]{1,0:T(2,128)(2,1)S(1)}, u32[]{:S(2)}, u32[]{:S(2)}) %collective-permute-start) | collective-permute-done | bytes 49184 | tf_op jit(solution)/shard_map/ppermute | solution.py:455
  79.9 7.0 %side.1 = (f32[128,4096]{1,0:T(8,128)}, bf16[128,4096]{1,0:T(8,128)(2,1)}) custom-call(bf16[128,12288]{1,0:T(8,128)(2,1)} %v_ref.1, bf16[128,12288]{1,0:T(8,128)(2,1)} %v_ref.1, bf16[128,12288]{1,0:T(8,128)(2,1)} %v_ref.1, bf16[2,12288]{1,0:T(2,128)(2,1)S(1)} %collective-permute-done.rq_ref.rk_ref.rv_ref, ...), custom_call_target="tpu_custom_call" | custom-call | tf_op jit(solution)/shard_map/side/pallas_call | solution.py:421
  86.9 0.0 all-to-all-done.1.c_ref
  86.9 0.0 copy-done.8
  86.9 0.0 copy-start
  86.9 1.6 %copy-done = f32[128,4096]{1,0:T(8,128)S(1)} copy-done((f32[128,4096]{1,0:T(8,128)S(1)}, f32[128,4096]{1,0:T(8,128)}, u32[]{:S(2)}) %copy-start) | copy-done | bytes 2097176
  88.5 2.4 %mix.1 = bf16[128,4096]{1,0:T(8,128)(2,1)} custom-call(bf16[128,32,128]{2,1,0:T(8,128)(2,1)S(1)} %all-to-all-done.1.c_ref, f32[128,4096]{1,0:T(8,128)S(1)} %copy-done, f32[1,4096]{1,0:T(1,128)S(1)} %bitcast.1, bf16[128,4096]{1,0:T(8,128)(2,1)} %get-tuple-element.8.g_ref), custom_call_target="tpu_custom_call" | custom-call | tf_op jit(solution)/shard_map/mix/pallas_call | solution.py:375
  (1 shorter events, 0.0 us)
Async XLA Ops:
  4.9 11.6 %copy-start.1 = (bf16[3,12288]{1,0:T(4,128)(2,1)S(1)}, bf16[3,12288]{1,0:T(4,128)(2,1)}, u32[]{:S(2)}) copy-start(bf16[3,12288]{1,0:T(4,128)(2,1)} %wv_ref.1) | copy-start | bytes 221188
  4.9 44.9 %copy-start.2 = (bf16[256,256]{1,0:T(8,128)(2,1)S(1)}, bf16[256,256]{1,0:T(8,128)(2,1)}, u32[]{:S(2)}) copy-start(bf16[256,256]{1,0:T(8,128)(2,1)} %constant.43.clone.bwd_ref) | copy-start | bytes 393220
  4.9 44.9 %copy-start.3 = (bf16[256,256]{1,0:T(8,128)(2,1)S(1)}, bf16[256,256]{1,0:T(8,128)(2,1)}, u32[]{:S(2)}) copy-start(bf16[256,256]{1,0:T(8,128)(2,1)} %constant.42.clone.fwd_ref) | copy-start | bytes 393220
  4.9 44.9 %copy-start.4 = (f32[128,128]{1,0:T(8,128)S(1)}, f32[128,128]{1,0:T(8,128)}, u32[]{:S(2)}) copy-start(f32[128,128]{1,0:T(8,128)} %constant.46.clone.ts_ref) | copy-start | bytes 196612
  4.9 44.9 %copy-start.5 = (f32[128,128]{1,0:T(8,128)S(1)}, f32[128,128]{1,0:T(8,128)}, u32[]{:S(2)}) copy-start(f32[128,128]{1,0:T(8,128)} %constant.45.clone.tc_ref) | copy-start | bytes 196612
  4.9 44.9 %copy-start.6 = (bf16[128,256]{1,0:T(8,128)(2,1)S(1)}, bf16[128,256]{1,0:T(8,128)(2,1)}, u32[]{:S(2)}) copy-start(bf16[128,256]{1,0:T(8,128)(2,1)} %constant.44.clone.last_ref) | copy-start | bytes 196612
  4.9 44.9 %copy-start.7 = (bf16[256,128]{1,0:T(8,128)(2,1)S(1)}, bf16[256,128]{1,0:T(8,128)(2,1)}, u32[]{:S(2)}) copy-start(bf16[256,128]{1,0:T(8,128)(2,1)} %constant.41.clone.first_ref) | copy-start | bytes 196612
  4.9 44.9 %copy-start.9 = (f32[1,128]{1,0:T(1,128)S(1)}, f32[1,128]{1,0:T(1,128)}, u32[]{:S(2)}) copy-start(f32[1,128]{1,0:T(1,128)} %constant.48.clone.hs_ref) | copy-start | bytes 1540
  5.0 44.9 %copy-start.10 = (f32[1,128]{1,0:T(1,128)S(1)}, f32[1,128]{1,0:T(1,128)}, u32[]{:S(2)}) copy-start(f32[1,128]{1,0:T(1,128)} %constant.47.clone.hc_ref) | copy-start | bytes 1540
  5.0 44.8 %all-to-all-start = ((bf16[128,72,128]{2,1,0:T(8,128)(2,1)}), bf16[128,72,128]{2,1,0:T(8,128)(2,1)S(1)}, u32[]{:S(2)}, u32[]{:S(2)}) async-start(bf16[128,72,128]{2,1,0:T(8,128)(2,1)} %gate.1), calls=%async_computation | async-start | bytes 4718592 | tf_op jit(solution)/shard_map/all_to_all | solution.py:454
  56.3 30.6 %all-to-all-start.1 = ((bf16[128,32,128]{2,1,0:T(8,128)(2,1)}), bf16[128,32,128]{2,1,0:T(8,128)(2,1)S(1)}, u32[]{:S(2)}, u32[]{:S(2)}) async-start(bf16[128,32,128]{2,1,0:T(8,128)(2,1)} %spectral.1), calls=%async_computation.1 | async-start | bytes 2097152 | tf_op jit(solution)/shard_map/all_to_all | solution.py:458
  61.9 25.0 %copy-start.8 = (f32[4096]{0:T(1024)S(1)}, f32[4096]{0:T(1024)}, u32[]{:S(2)}) copy-start(f32[4096]{0:T(1024)} %param.15) | copy-start | bytes 49156
  61.9 18.0 %collective-permute-start = (bf16[2,12288]{1,0:T(2,128)(2,1)S(1)}, bf16[2,12288]{1,0:T(2,128)(2,1)S(1)}, u32[]{:S(2)}, u32[]{:S(2)}) collective-permute-start(bf16[2,12288]{1,0:T(2,128)(2,1)S(1)} %slice.3), channel_id=1, source_target_pairs={{0,1},{1,2},{2,3},{3,4},{4,5},{5,6},{6,7},{7,8},{8,9},{9,10},{10,1... | collective-permute-start | bytes 147464 | tf_op jit(solution)/shard_map/ppermute | solution.py:455
  86.9 1.6 %copy-start = (f32[128,4096]{1,0:T(8,128)S(1)}, f32[128,4096]{1,0:T(8,128)}, u32[]{:S(2)}) copy-start(f32[128,4096]{1,0:T(8,128)} %get-tuple-element.7.q_ref) | copy-start | bytes 6291460

commit v5 on v4

--- a/solution.py
+++ b/solution.py
@@ -335,30 +335,23 @@
     )(resident(received), taps, *consts)
 
 
-def mix_kernel(c_ref, q_ref, skip_ref, g_ref, out_ref, g_buf, buf_ref, sem):
+def mix_kernel(c_ref, q_ref, skip_ref, g_ref, out_ref, buf_ref, sem):
     peers, own, tok = c_ref.shape
     steps = sem.shape[0]
     peers = peers // steps
     cols = peers * own
     near = 128 // own
 
-    def read(i):
-        at = pl.ds(i * cols, cols)
-        return pltpu.make_async_copy(g_ref.at[:, at], g_buf.at[:, at], sem.at[i, 0])
-
     def write(i):
         at = pl.ds(i * cols, cols)
-        return pltpu.make_async_copy(buf_ref.at[:, at], out_ref.at[:, at], sem.at[i, 1])
+        return pltpu.make_async_copy(buf_ref.at[:, at], out_ref.at[:, at], sem.at[i])
 
     for i in range(steps):
-        read(i).start()
-    for i in range(steps):
-        read(i).wait()
         for j in range(i * peers, (i + 1) * peers, near):
             at = slice(j * own, (j + near) * own)
             conv = c_ref[j : j + near].reshape(near * own, tok).T.astype(F32)
-            direct = skip_ref[:, at] * g_buf[:, at].astype(F32)
-            buf_ref[:, at] = (q_ref[:, at] * (conv + direct)).astype(BF16)
+            direct = skip_ref[:, at] * g_ref[:, at].astype(F32)
+            buf_ref[:, at] = (q_ref[:, at].astype(F32) * (conv + direct)).astype(BF16)
         write(i).start()
     for i in range(steps):
         write(i).wait()
@@ -374,18 +367,16 @@
     steps = 8
     return pl.pallas_call(
         mix_kernel,
-        in_specs=[pl.BlockSpec(memory_space=pltpu.VMEM)] * 3
-        + [pl.BlockSpec(memory_space=pltpu.HBM)],
+        in_specs=[pl.BlockSpec(memory_space=pltpu.VMEM)] * 4,
         out_specs=pl.BlockSpec(memory_space=pltpu.HBM),
         out_shape=jax.ShapeDtypeStruct((tok, width), BF16),
         scratch_shapes=[
             pltpu.VMEM((tok, width), BF16),
-            pltpu.VMEM((tok, width), BF16),
-            pltpu.SemaphoreType.DMA((steps, 2)),
+            pltpu.SemaphoreType.DMA((steps,)),
         ],
         compiler_params=pltpu.CompilerParams(vmem_limit_bytes=6 << 20),
         name="mix",
-    )(resident(conv), resident(query), resident(skip), in_hbm(gated))
+    )(resident(conv), resident(query), resident(skip), resident(gated))
 
 
 def side_kernel(q_ref, k_ref, v_ref, rq_ref, rk_ref, rv_ref, wq_ref, wk_ref, wv_ref,
@@ -400,7 +391,7 @@
         back2 = jnp.where(index == 0, rim[0:1], jnp.where(index == 1, rim[1:2], back2))
         return taps[0:1] * rows + taps[1:2] * back1 + taps[2:3] * back2
 
-    query_ref[...] = featurized(q_ref, rq_ref, wq_ref)
+    query_ref[...] = featurized(q_ref, rq_ref, wq_ref).astype(BF16)
     gated = featurized(k_ref, rk_ref, wk_ref) * featurized(v_ref, rv_ref, wv_ref)
     gated_ref[...] = gated.astype(BF16)
 
@@ -426,8 +417,8 @@
         + thirds(short_filter.shape[0]),
         out_specs=[wide, wide],
         out_shape=[
-            pltpu.HBM((tok, width), F32),
-            pltpu.HBM((tok, width), BF16),
+            jax.ShapeDtypeStruct((tok, width), BF16),
+            jax.ShapeDtypeStruct((tok, width), BF16),
         ],
         compiler_params=pltpu.CompilerParams(vmem_limit_bytes=8 << 20),
         name="side",

time: 91.4 us -> 87.6 us (0.958)
  Pallas kernels: 20.8 us -> 18.5 us
  local copies, waits for them, and re-layouts: 2.71 us -> 1.13 us
    unnamed x22 -> x20, local copies, waits for them, and re-layouts: 1.65 us -> 0.07 us
    pallas_call x1, Pallas kernels: 2.44 us -> 1.24 us  [mix(): pl.pallas_call(mix_kernel, in_specs=[pl.BlockSpec(memory_space=pltpu.VMEM...]
    pallas_call x1, Pallas kernels: 7.03 us -> 6 us  [side(): pl.pallas_call(side_kernel, grid=(steps,), in_specs=thirds(tok) + thirds(...]
  transfers between devices with their start and end apart: 3 -> 3, of which waited for: 2 -> 2; matrix products, arithmetic and copies ran while one was open for 1% -> 1% of each run, Pallas kernels for 8% -> 7%
where the time goes in v5:
time: 87.6 us; the launch traced here: 87.1 us
  waiting for transfers between devices  47.9 us (55%)
  starting transfers between devices  19.4 us (22%)
  Pallas kernels  18.5 us (21%)
  local copies, waits for them, and re-layouts  1.13 us (1%)
    all_to_all x1, waiting for transfers between devices, shards(): lax.all_to_all(send, AXES, split_axis=0, concat_axis=0, tiled=True)  33.2 us
    ppermute x1, waiting for transfers between devices, shards(): lax.ppermute(projected[tok - rim_count:], AXES, [(i, i + 1) for i in rang...  14.7 us
    all_to_all x1, starting transfers between devices, shards(): lax.all_to_all(send, AXES, split_axis=0, concat_axis=0, tiled=True)  11.5 us
    pallas_call x1, Pallas kernels, spectral(): pl.pallas_call(spectral_kernel, out_shape=pltpu.HBM((segments, own, tok),...  6.45 us
    pallas_call x1, Pallas kernels, side(): pl.pallas_call(side_kernel, grid=(steps,), in_specs=thirds(tok) + thirds(...  6 us
    pallas_call x1, Pallas kernels, gate(): pl.pallas_call(gate_kernel, in_specs=[pl.BlockSpec(memory_space=pltpu.HBM...  4.86 us
    all_to_all x1, starting transfers between devices, shards(): conv = lax.all_to_all(conv, AXES, split_axis=0, concat_axis=0, tiled=True)  4.61 us
    ppermute x1, starting transfers between devices, shards(): lax.ppermute(projected[tok - rim_count:], AXES, [(i, i + 1) for i in rang...  3.28 us
  transfers between devices with their start and end apart: 3, of which 2 were waited for; matrix products, arithmetic and copies ran while one was open for 1% of the time, Pallas kernels for 7%

profile of v5, /device:TPU:1, one launch (start us, length us, event | category | flops | bytes accessed | tf_op | source)
XLA Modules:
  0.0 87.1 jit_solution(14090284358845011797)
XLA Ops:
  0.0 4.9 %gate.1 = bf16[128,72,128]{2,1,0:T(8,128)(2,1)} custom-call(bf16[128,12288]{1,0:T(8,128)(2,1)} %v_ref.1, bf16[128,4096]{1,0:T(8,128)(2,1)} %f_ref.1, bf16[3,12288]{1,0:T(4,128)(2,1)} %wv_ref.1), custom_call_target="tpu_custom_call" | custom-call | tf_op jit(solution)/shard_map/gate/pallas_call | solution.py:141
  4.9 0.0 copy-start
  4.9 0.0 copy-start.1
  4.9 0.0 copy-start.2
  4.9 0.0 copy-start.3
  4.9 0.0 copy-start.4
  4.9 0.0 copy-start.5
  4.9 0.0 copy-start.6
  5.0 0.0 copy-start.8
  5.0 0.0 copy-start.9
  5.0 11.5 %all-to-all-start = ((bf16[128,72,128]{2,1,0:T(8,128)(2,1)}), bf16[128,72,128]{2,1,0:T(8,128)(2,1)S(1)}, u32[]{:S(2)}, u32[]{:S(2)}) async-start(bf16[128,72,128]{2,1,0:T(8,128)(2,1)} %gate.1), calls=%async_computation | async-start | bytes 4718592 | tf_op jit(solution)/shard_map/all_to_all | solution.py:445
  16.5 0.0 copy-done
  16.5 0.1 constant_dynamic-slice_fusion.1
  16.6 33.2 %all-to-all-done.z_ref = bf16[128,72,128]{2,1,0:T(8,128)(2,1)S(1)} async-done(((bf16[128,72,128]{2,1,0:T(8,128)(2,1)}), bf16[128,72,128]{2,1,0:T(8,128)(2,1)S(1)}, u32[]{:S(2)}, u32[]{:S(2)}) %all-to-all-start) | async-done | bytes 2359328 | tf_op jit(solution)/shard_map/all_to_all | solution.py:445
  49.8 0.0 copy-done.1
  49.8 0.0 copy-done.2
  49.8 0.0 copy-done.3
  49.8 0.0 copy-done.4
  49.8 0.0 copy-done.5
  49.8 0.0 copy-done.6
  49.8 0.0 copy-done.8
  49.8 0.0 copy-done.9
  49.8 6.5 %spectral.1 = bf16[128,32,128]{2,1,0:T(8,128)(2,1)} custom-call(bf16[128,72,128]{2,1,0:T(8,128)(2,1)S(1)} %all-to-all-done.z_ref, f32[8,128]{1,0:T(8,128)S(1)} %fusion.6.taps_ref, bf16[256,128]{1,0:T(8,128)(2,1)S(1)} %copy-done.3, bf16[256,256]{1,0:T(8,128)(2,1)S(1)} %copy-done.1, bf16[256,256]{1,0:T(8,128)(2,1)S(1)} %copy-done.2, ...), custom_call_target="tpu_custom_call" | custom-call | tf_op jit(solution)/shard_map/spectral/pallas_call | solution.py:316
  56.3 4.6 %all-to-all-start.1 = ((bf16[128,32,128]{2,1,0:T(8,128)(2,1)}), bf16[128,32,128]{2,1,0:T(8,128)(2,1)S(1)}, u32[]{:S(2)}, u32[]{:S(2)}) async-start(bf16[128,32,128]{2,1,0:T(8,128)(2,1)} %spectral.1), calls=%async_computation.1 | async-start | bytes 2097152 | tf_op jit(solution)/shard_map/all_to_all | solution.py:449
  60.9 1.0 %slice.3 = bf16[2,12288]{1,0:T(2,128)(2,1)S(1)} slice(bf16[128,12288]{1,0:T(8,128)(2,1)} %v_ref.1), slice={[126:128], [0:12288]} | slice | bytes 98304 | tf_op jit(solution)/shard_map/slice | solution.py:446
  61.9 0.0 copy-start.7
  61.9 3.3 %collective-permute-start = (bf16[2,12288]{1,0:T(2,128)(2,1)S(1)}, bf16[2,12288]{1,0:T(2,128)(2,1)S(1)}, u32[]{:S(2)}, u32[]{:S(2)}) collective-permute-start(bf16[2,12288]{1,0:T(2,128)(2,1)S(1)} %slice.3), channel_id=1, source_target_pairs={{0,1},{1,2},{2,3},{3,4},{4,5},{5,6},{6,7},{7,8},{8,9},{9,10},{10,1... | collective-permute-start | bytes 147464 | tf_op jit(solution)/shard_map/ppermute | solution.py:446
  65.2 14.7 %collective-permute-done.rq_ref.rk_ref.rv_ref = bf16[2,12288]{1,0:T(2,128)(2,1)S(1)} collective-permute-done((bf16[2,12288]{1,0:T(2,128)(2,1)S(1)}, bf16[2,12288]{1,0:T(2,128)(2,1)S(1)}, u32[]{:S(2)}, u32[]{:S(2)}) %collective-permute-start) | collective-permute-done | bytes 49184 | tf_op jit(solution)/shard_map/ppermute | solution.py:446
  79.9 6.0 %side.1 = (bf16[128,4096]{1,0:T(8,128)(2,1)S(1)}, bf16[128,4096]{1,0:T(8,128)(2,1)S(1)}) custom-call(bf16[128,12288]{1,0:T(8,128)(2,1)} %v_ref.1, bf16[128,12288]{1,0:T(8,128)(2,1)} %v_ref.1, bf16[128,12288]{1,0:T(8,128)(2,1)} %v_ref.1, bf16[2,12288]{1,0:T(2,128)(2,1)S(1)} %collective-permute-done.rq_ref.rk_ref.rv_ref, ...), custom_call_target="tpu_custom_call" | custom-call | tf_op jit(solution)/shard_map/side/pallas_call | solution.py:412
  85.9 0.0 all-to-all-done.1.c_ref
  85.9 0.0 copy-done.7
  85.9 1.2 %mix.1 = bf16[128,4096]{1,0:T(8,128)(2,1)} custom-call(bf16[128,32,128]{2,1,0:T(8,128)(2,1)S(1)} %all-to-all-done.1.c_ref, bf16[128,4096]{1,0:T(8,128)(2,1)S(1)} %get-tuple-element.7.q_ref, f32[1,4096]{1,0:T(1,128)S(1)} %bitcast.1, bf16[128,4096]{1,0:T(8,128)(2,1)S(1)} %get-tuple-element.8.g_ref), custom_call_target="tpu_custom_call" | custom-call | tf_op jit(solution)/shard_map/mix/pallas_call | solution.py:368
  (1 shorter events, 0.0 us)
Async XLA Ops:
  4.9 11.6 %copy-start = (bf16[3,12288]{1,0:T(4,128)(2,1)S(1)}, bf16[3,12288]{1,0:T(4,128)(2,1)}, u32[]{:S(2)}) copy-start(bf16[3,12288]{1,0:T(4,128)(2,1)} %wv_ref.1) | copy-start | bytes 221188
  4.9 44.9 %copy-start.1 = (bf16[256,256]{1,0:T(8,128)(2,1)S(1)}, bf16[256,256]{1,0:T(8,128)(2,1)}, u32[]{:S(2)}) copy-start(bf16[256,256]{1,0:T(8,128)(2,1)} %constant.42.clone.fwd_ref) | copy-start | bytes 393220
  4.9 44.9 %copy-start.2 = (bf16[256,256]{1,0:T(8,128)(2,1)S(1)}, bf16[256,256]{1,0:T(8,128)(2,1)}, u32[]{:S(2)}) copy-start(bf16[256,256]{1,0:T(8,128)(2,1)} %constant.43.clone.bwd_ref) | copy-start | bytes 393220
  4.9 44.9 %copy-start.3 = (bf16[256,128]{1,0:T(8,128)(2,1)S(1)}, bf16[256,128]{1,0:T(8,128)(2,1)}, u32[]{:S(2)}) copy-start(bf16[256,128]{1,0:T(8,128)(2,1)} %constant.41.clone.first_ref) | copy-start | bytes 196612
  4.9 44.9 %copy-start.4 = (bf16[128,256]{1,0:T(8,128)(2,1)S(1)}, bf16[128,256]{1,0:T(8,128)(2,1)}, u32[]{:S(2)}) copy-start(bf16[128,256]{1,0:T(8,128)(2,1)} %constant.44.clone.last_ref) | copy-start | bytes 196612
  4.9 44.9 %copy-start.5 = (f32[128,128]{1,0:T(8,128)S(1)}, f32[128,128]{1,0:T(8,128)}, u32[]{:S(2)}) copy-start(f32[128,128]{1,0:T(8,128)} %constant.45.clone.tc_ref) | copy-start | bytes 196612
  4.9 44.9 %copy-start.6 = (f32[128,128]{1,0:T(8,128)S(1)}, f32[128,128]{1,0:T(8,128)}, u32[]{:S(2)}) copy-start(f32[128,128]{1,0:T(8,128)} %constant.46.clone.ts_ref) | copy-start | bytes 196612
  5.0 44.9 %copy-start.8 = (f32[1,128]{1,0:T(1,128)S(1)}, f32[1,128]{1,0:T(1,128)}, u32[]{:S(2)}) copy-start(f32[1,128]{1,0:T(1,128)} %constant.47.clone.hc_ref) | copy-start | bytes 1540
  5.0 44.9 %copy-start.9 = (f32[1,128]{1,0:T(1,128)S(1)}, f32[1,128]{1,0:T(1,128)}, u32[]{:S(2)}) copy-start(f32[1,128]{1,0:T(1,128)} %constant.48.clone.hs_ref) | copy-start | bytes 1540
  5.0 44.8 %all-to-all-start = ((bf16[128,72,128]{2,1,0:T(8,128)(2,1)}), bf16[128,72,128]{2,1,0:T(8,128)(2,1)S(1)}, u32[]{:S(2)}, u32[]{:S(2)}) async-start(bf16[128,72,128]{2,1,0:T(8,128)(2,1)} %gate.1), calls=%async_computation | async-start | bytes 4718592 | tf_op jit(solution)/shard_map/all_to_all | solution.py:445
  56.3 29.6 %all-to-all-start.1 = ((bf16[128,32,128]{2,1,0:T(8,128)(2,1)}), bf16[128,32,128]{2,1,0:T(8,128)(2,1)S(1)}, u32[]{:S(2)}, u32[]{:S(2)}) async-start(bf16[128,32,128]{2,1,0:T(8,128)(2,1)} %spectral.1), calls=%async_computation.1 | async-start | bytes 2097152 | tf_op jit(solution)/shard_map/all_to_all | solution.py:449
  61.9 24.0 %copy-start.7 = (f32[4096]{0:T(1024)S(1)}, f32[4096]{0:T(1024)}, u32[]{:S(2)}) copy-start(f32[4096]{0:T(1024)} %param.15) | copy-start | bytes 49156
  61.9 18.0 %collective-permute-start = (bf16[2,12288]{1,0:T(2,128)(2,1)S(1)}, bf16[2,12288]{1,0:T(2,128)(2,1)S(1)}, u32[]{:S(2)}, u32[]{:S(2)}) collective-permute-start(bf16[2,12288]{1,0:T(2,128)(2,1)S(1)} %slice.3), channel_id=1, source_target_pairs={{0,1},{1,2},{2,3},{3,4},{4,5},{5,6},{6,7},{7,8},{8,9},{9,10},{10,1... | collective-permute-start | bytes 147464 | tf_op jit(solution)/shard_map/ppermute | solution.py:446

commit v6 on v5

--- a/solution.py
+++ b/solution.py
@@ -11,6 +11,7 @@
 
 
 AXES = ("outer", "inner")
+TURNED = ("inner", "outer")
 F32 = jnp.float32
 BF16 = jnp.bfloat16
 PAD = 1
@@ -28,12 +29,13 @@
     return both.reshape(-1, reals.shape[1])
 
 
-def tables(segments, tok):
+def tables(order, tok):
+    segments = len(order)
     half = segments
     blocks = 2 * segments
     transform = blocks * tok
     kb = np.arange(half + 1)
-    cos_b, sin_b = turn_table(kb[:, None], np.arange(segments)[None, :], blocks)
+    cos_b, sin_b = turn_table(kb[:, None], np.asarray(order)[None, :], blocks)
     first = paired(cos_b[:half], np.concatenate([cos_b[half:], -sin_b[1:half]], 0))
     weight = np.full((half + 1,), 2.0, np.float32)
     weight[0] = weight[half] = 1.0
@@ -56,20 +58,25 @@
     )
 
 
-EXTRA = 8
+EXTRA = 2
 
 
 def in_hbm(value):
     return pltpu.with_memory_space_constraint(value, pltpu.HBM)
 
 
-def gate_kernel(p_ref, f_ref, t_ref, send_ref, w_ref, k_buf, v_buf, f_buf, out_buf, k_ext, v_ext, e_ext, sem, tap_sem):
+def gate_kernel(
+    own, p_ref, f_ref, t_ref, send_ref, w_ref, k_buf, v_buf, f_buf, out_buf, k_ext, v_ext, e_ext,
+    stage, sem, tap_sem,
+):
     tok, width = f_ref.shape
-    devices, _, _ = send_ref.shape
-    own = width // devices
+    run = 2 * own + EXTRA
     steps = sem.shape[0]
     cols = width // steps
-    peers = devices // steps
+    lanes = e_ext.shape[2]
+    near = lanes // own
+    chunk = cols // own * run
+    ahead = 2
 
     def reads(i):
         at = pl.ds(i * cols, cols)
@@ -84,23 +91,27 @@
         )
 
     def write(i):
-        at = pl.ds(i * peers, peers)
+        at = pl.ds(i * chunk, chunk)
         return pltpu.make_async_copy(out_buf.at[at], send_ref.at[at], sem.at[i, 3])
 
     taps_read = pltpu.make_async_copy(t_ref, w_ref, tap_sem)
     taps_read.start()
-    for i in range(steps):
+    for i in range(ahead):
         for copy in reads(i):
             copy.start()
     lead = 8
-    lanes = k_ext.shape[2]
     for j in range(cols // lanes):
         k_ext[j, :lead] = jnp.zeros((lead, lanes), F32)
         v_ext[j, :lead] = jnp.zeros((lead, lanes), F32)
+    row = lax.broadcasted_iota(jnp.int32, (8, lanes), 0) % 4
+    piece = lax.broadcasted_iota(jnp.int32, (8, lanes), 1) // own
     taps_read.wait()
     for i in range(steps):
         for copy in reads(i):
             copy.wait()
+        if i + ahead < steps:
+            for copy in reads(i + ahead):
+                copy.start()
         for j in range(cols // lanes):
             start = i * cols + j * lanes
             at = slice(start, start + lanes)
@@ -115,18 +126,28 @@
                 )
 
             gated = featurized(k_buf, k_ext, width) * featurized(v_buf, v_ext, 2 * width)
-            near = lanes // own
-            to = slice(start // own, start // own + near)
-            out_buf[to, :own] = gated.astype(BF16).T.reshape(near, own, tok)
-            out_buf[to, own : 2 * own] = f_buf[:, at].T.reshape(near, own, tok)
-            e_ext[0:2] = k_ext[j, lead : lead + 2]
-            e_ext[2:4] = v_ext[j, lead : lead + 2]
-            e_ext[4:6] = k_ext[j, lead + tok - 2 : lead + tok]
-            e_ext[6:8] = v_ext[j, lead + tok - 2 : lead + tok]
-            tile = e_ext[...]
+            gated = gated.astype(BF16).T.astype(F32)
+            taken = f_buf[:, at].T.astype(F32)
+            e_ext[j, 0:2] = k_ext[j, lead : lead + 2]
+            e_ext[j, 2:4] = v_ext[j, lead : lead + 2]
+            e_ext[j, 4:6] = k_ext[j, lead + tok - 2 : lead + tok]
+            e_ext[j, 6:8] = v_ext[j, lead + tok - 2 : lead + tok]
+            edge = e_ext[j]
+            turned = edge
+            for m in range(1, near):
+                turned = jnp.where(row == m, pltpu.roll(edge, m * own, 1), turned)
             for k in range(near):
-                turned = pltpu.roll(tile, lanes - k * own, 1) if k else tile
-                out_buf[start // own + k, 2 * own :] = turned.astype(BF16)
+                to = (j * near + k) * run
+                mine = slice(k * own, (k + 1) * own)
+                stage[i % 2, to : to + own, :] = gated[mine]
+                stage[i % 2, to + own : to + 2 * own, :] = taken[mine]
+                part = pltpu.roll(turned, lanes - k * own, 1) if k else turned
+                part = jnp.where(row == piece, part, 0.0)
+                part = part + pltpu.roll(part, 7, 0)
+                part = part + pltpu.roll(part, 6, 0)
+                stage[i % 2, to + 2 * own : to + 2 * own + 1, :] = part[0:1]
+                stage[i % 2, to + 2 * own + 1 : to + 2 * own + 2, :] = part[4:5]
+        out_buf[i * chunk : (i + 1) * chunk] = stage[i % 2].astype(BF16)
         write(i).start()
     for i in range(steps):
         write(i).wait()
@@ -137,29 +158,26 @@
     own = width // devices
     steps = 8
     cols = width // steps
-    rows = 2 * own + EXTRA
+    run = 2 * own + EXTRA
     return pl.pallas_call(
-        gate_kernel,
-        in_specs=[
-            pl.BlockSpec(memory_space=pltpu.HBM),
-            pl.BlockSpec(memory_space=pltpu.HBM),
-            pl.BlockSpec(memory_space=pltpu.HBM),
-        ],
+        functools.partial(gate_kernel, own),
+        in_specs=[pl.BlockSpec(memory_space=pltpu.HBM)] * 3,
         out_specs=pl.BlockSpec(memory_space=pltpu.HBM),
-        out_shape=pltpu.HBM((devices, rows, tok), BF16),
+        out_shape=pltpu.HBM((devices * run, tok), BF16),
         scratch_shapes=[
             pltpu.VMEM(short_filter.shape, BF16),
             pltpu.VMEM((tok, width), BF16),
             pltpu.VMEM((tok, width), BF16),
             pltpu.VMEM((tok, width), BF16),
-            pltpu.VMEM((devices, rows, tok), BF16),
+            pltpu.VMEM((devices * run, tok), BF16),
             pltpu.VMEM((cols // 128, tok + 8, 128), F32),
             pltpu.VMEM((cols // 128, tok + 8, 128), F32),
-            pltpu.VMEM((EXTRA, 128), F32),
+            pltpu.VMEM((cols // 128, 8, 128), F32),
+            pltpu.VMEM((2, cols // own * run, 128), F32),
             pltpu.SemaphoreType.DMA((steps, 4)),
             pltpu.SemaphoreType.DMA(()),
         ],
-        compiler_params=pltpu.CompilerParams(vmem_limit_bytes=16 << 20),
+        compiler_params=pltpu.CompilerParams(vmem_limit_bytes=20 << 20),
         name="gate",
     )(in_hbm(projected), in_hbm(long_filter), in_hbm(short_filter))
 
@@ -169,45 +187,39 @@
 
 
 def spectral_kernel(
-    z_ref, taps_ref, first_ref, fwd_ref, bwd_ref, last_ref, tc_ref, ts_ref, hc_ref, hs_ref,
+    outer, z_ref, taps_ref, first_ref, fwd_ref, bwd_ref, last_ref, tc_ref, ts_ref, hc_ref, hs_ref,
     out_ref, rows_ref, fix_ref, spec_ref, half_ref, half_out_ref, prod_ref, back_ref, conv_ref, block_ref, sem,
 ):
-    segments, rows, tok = z_ref.shape
-    both = rows - EXTRA
-    own = both // 2
-    pitch = rows_ref.shape[0] // (segments + 1)
+    segments, own, tok = out_ref.shape
+    both = 2 * own
+    pitch = both + EXTRA
     out_pitch = conv_ref.shape[0] // segments
     piece = 16
+    rim = outer * pitch
 
     def widen(i, carry):
-        for j in range(piece):
-            b = i * piece + j
-            rows_ref[pl.ds((b + 1) * pitch, rows), :] = z_ref[b].astype(F32)
+        start = pl.multiple_of(i * (piece * pitch), piece * pitch)
+        block = z_ref[pl.ds(start, piece * pitch), :].astype(F32)
+        rows_ref[pl.ds(rim + start, piece * pitch), :] = block
         return carry
 
     lax.fori_loop(0, segments // piece, widen, 0)
 
-    rows_ref[both:rows, :] = jnp.zeros((EXTRA, tok), F32)
-
-    def sent(row, before):
-        return rows_ref[pl.ds(both + row + (1 - before) * pitch, segments, stride=pitch), :]
-
-    def edge(tap, at):
-        now0, now1 = sent(at, 0), sent(at + 1, 0)
-        ago2, ago1 = sent(at + 4, 1), sent(at + 5, 1)
-        taps = [taps_ref[tap + n : tap + n + 1, :] for n in range(3)]
-        return (
-            taps[0] * now0 + taps[1] * ago1 + taps[2] * ago2,
-            taps[0] * now1 + taps[1] * now0 + taps[2] * ago1,
-        )
-
-    key0, key1 = edge(0, 0)
-    value0, value1 = edge(3, 2)
-    gated0 = key0 * value0
-    gated1 = pltpu.roll(key1 * value1, 1, 1)
+    rows_ref[pitch - 1 : pitch, :] = jnp.zeros((1, tok), F32)
+    for o in range(1, outer):
+        last = (segments + o - 1) * pitch + pitch - 1
+        rows_ref[o * pitch + pitch - 1 : (o + 1) * pitch, :] = rows_ref[last : last + 1, :]
+    now = rows_ref[pl.ds(rim + both, segments, stride=pitch), :]
+    ago = rows_ref[pl.ds(both + 1, segments, stride=pitch), :]
     lane = lax.broadcasted_iota(jnp.int32, (segments, tok), 1)
-    fix_ref[0] = jnp.where(lane % 2 == 0, gated0, gated1)
-    fix_ref[1] = jnp.where(lane % 2 == 1, gated0, gated1)
+    middle = jnp.where(
+        lane // own % 2 == 0, pltpu.roll(ago, tok - own, 1), pltpu.roll(now, own, 1)
+    )
+    edges = taps_ref[0:1, :] * now + taps_ref[1:2, :] * middle + taps_ref[2:3, :] * ago
+    edges = edges * pltpu.roll(edges, tok - 2 * own, 1)
+    after = pltpu.roll(edges, tok - own + 1, 1)
+    fix_ref[0] = jnp.where(lane % 2 == 0, edges, after)
+    fix_ref[1] = jnp.where(lane % 2 == 1, edges, after)
 
     top = 8
     index = lax.broadcasted_iota(jnp.int32, (top, tok), 0)
@@ -224,7 +236,7 @@
         base = which * own + start
         cols = []
         for j in range(group):
-            col = rows_ref[pl.ds(base + j + pitch, segments, stride=pitch), :]
+            col = rows_ref[pl.ds(rim + base + j, segments, stride=pitch), :]
             if which == 0:
                 fixed = pltpu.roll(fix_ref[j % 2], (tok - start - j) % tok, 1)
                 col = jnp.where(lane < 2, fixed, col)
@@ -309,17 +321,18 @@
         write(i).wait()
 
 
-def spectral(received, taps, consts):
-    segments, rows, tok = received.shape
-    both = rows - EXTRA
-    own = both // 2
+def spectral(received, taps, consts, outer, own):
+    tok = received.shape[1]
+    both = 2 * own
+    pitch = both + EXTRA
+    segments = received.shape[0] // pitch
     return pl.pallas_call(
-        spectral_kernel,
+        functools.partial(spectral_kernel, outer),
         out_shape=pltpu.HBM((segments, own, tok), BF16),
         in_specs=[pl.BlockSpec(memory_space=pltpu.VMEM)] * 10,
         out_specs=pl.BlockSpec(memory_space=pltpu.HBM),
         scratch_shapes=[
-            pltpu.VMEM(((segments + 1) * (rows + PAD), tok), F32),
+            pltpu.VMEM(((segments + outer) * pitch, tok), F32),
             pltpu.VMEM((2, segments, tok), F32),
             pltpu.VMEM((own, segments // 16, 2, 16, 2 * tok), BF16),
             pltpu.VMEM((both, tok), F32),
@@ -431,22 +444,23 @@
     own = width // devices
     tap_count = short_filter.shape[0]
     rim_count = tap_count - 1
-    consts = tables(devices, tok)
-    position = lax.axis_index(AXES)
-    taps = jnp.concatenate(
-        [
-            lax.dynamic_slice_in_dim(short_filter, third * width + position * own, own, 1)
-            for third in (1, 2)
-        ],
-        0,
-    ).astype(F32)
-    taps = jnp.pad(taps, ((0, 8 - 2 * tap_count), (0, tok - own)))
+    outer = lax.axis_size("outer")
+    order = np.arange(devices).reshape(outer, -1).T.reshape(-1)
+    consts = tables(order, tok)
+    position = lax.axis_index(TURNED)
+    taps = [
+        lax.dynamic_slice_in_dim(short_filter, third * width + position * own, own, 1)
+        for third in (1, 2)
+    ]
+    taps = jnp.concatenate([taps[0], taps[0], taps[1], taps[1]], 1).astype(F32)
     send = gate(projected, short_filter, long_filter, devices)
-    received = lax.all_to_all(send, AXES, split_axis=0, concat_axis=0, tiled=True)
+    pairs = send.reshape(devices, -1, 2, tok)
+    received = lax.all_to_all(pairs, TURNED, split_axis=0, concat_axis=0, tiled=True)
+    received = received.reshape(send.shape)
     rim = lax.ppermute(projected[tok - rim_count :], AXES, [(i, i + 1) for i in range(devices - 1)])
     query, gated = side(projected, rim, short_filter)
-    conv = spectral(received, taps, consts)
-    conv = lax.all_to_all(conv, AXES, split_axis=0, concat_axis=0, tiled=True)
+    conv = spectral(received, taps, consts, outer, own)
+    conv = lax.all_to_all(conv, TURNED, split_axis=0, concat_axis=0, tiled=True)
     return mix(conv, query, skip[None, :], gated)
 
 

time: 87.6 us -> 86.6 us (0.989)
  waiting for transfers between devices: 47.9 us -> 45.2 us
  Pallas kernels: 18.5 us -> 20 us
    all_to_all x2, waiting for transfers between devices: 33.2 us -> 30.5 us  [the longest x1 30.5 us: shards(): lax.all_to_all(pairs, TURNED, split_axis=0, concat_axis=0, tiled=True)]
    pallas_call x2, Pallas kernels: 11.3 us -> 12.7 us  [the longest x1 6.58 us: spectral(): pl.pallas_call(functools.partial(spectral_kernel, outer), out_shape=pltpu...]
where the time goes in v6:
time: 86.6 us; the launch traced here: 86 us
  waiting for transfers between devices  45.2 us (52%)
  Pallas kernels  20 us (23%)
  starting transfers between devices  19.5 us (23%)
  local copies, waits for them, and re-layouts  1.13 us (1%)
    all_to_all x1, waiting for transfers between devices, shards(): lax.all_to_all(pairs, TURNED, split_axis=0, concat_axis=0, tiled=True)  30.5 us
    ppermute x1, waiting for transfers between devices, shards(): lax.ppermute(projected[tok - rim_count:], AXES, [(i, i + 1) for i in rang...  14.7 us
    all_to_all x1, starting transfers between devices, shards(): lax.all_to_all(pairs, TURNED, split_axis=0, concat_axis=0, tiled=True)  11.5 us
    pallas_call x1, Pallas kernels, spectral(): pl.pallas_call(functools.partial(spectral_kernel, outer), out_shape=pltpu...  6.58 us
    pallas_call x1, Pallas kernels, gate(): pl.pallas_call(functools.partial(gate_kernel, own), in_specs=[pl.BlockSpe...  6.16 us
    pallas_call x1, Pallas kernels, side(): pl.pallas_call(side_kernel, grid=(steps,), in_specs=thirds(tok) + thirds(...  6 us
    all_to_all x1, starting transfers between devices, shards(): conv = lax.all_to_all(conv, TURNED, split_axis=0, concat_axis=0, tiled=True)  4.7 us
    ppermute x1, starting transfers between devices, shards(): lax.ppermute(projected[tok - rim_count:], AXES, [(i, i + 1) for i in rang...  3.28 us
  transfers between devices with their start and end apart: 3, of which 2 were waited for; matrix products, arithmetic and copies ran while one was open for 1% of the time, Pallas kernels for 7%

profile of v6, /device:TPU:1, one launch (start us, length us, event | category | flops | bytes accessed | tf_op | source)
XLA Modules:
  0.0 86.0 jit_solution(10164430253569125077)
XLA Ops:
  0.0 6.2 %gate.1 = bf16[8448,128]{1,0:T(8,128)(2,1)} custom-call(bf16[128,12288]{1,0:T(8,128)(2,1)} %v_ref.1, bf16[128,4096]{1,0:T(8,128)(2,1)} %f_ref.1, bf16[3,12288]{1,0:T(4,128)(2,1)} %wv_ref.1), custom_call_target="tpu_custom_call" | custom-call | tf_op jit(solution)/shard_map/gate/pallas_call | solution.py:162
  6.2 0.0 copy-start
  6.2 0.0 copy-start.1
  6.2 0.0 copy-start.2
  6.2 0.0 copy-start.3
  6.2 0.0 copy-start.4
  6.2 0.0 copy-start.5
  6.2 0.0 copy-start.6
  6.3 0.0 copy-start.8
  6.3 0.0 copy-start.9
  6.3 11.5 %all-to-all-start = ((bf16[128,33,2,128]{3,2,1,0:T(2,128)(2,1)}), bf16[128,33,2,128]{3,2,1,0:T(2,128)(2,1)S(1)}, u32[]{:S(2)}, u32[]{:S(2)}) async-start(bf16[128,33,2,128]{3,2,1,0:T(2,128)(2,1)} %bitcast.5), calls=%async_computation | async-start | bytes 4325376 | tf_op jit(solution)/shard_map/all_to_all | solution.py:458
  17.8 0.0 copy-done
  17.8 0.1 constant_dynamic-slice_fusion.1
  17.9 0.1 maximum_convert_fusion.taps_ref
  18.0 30.5 %all-to-all-done = bf16[128,33,2,128]{3,2,1,0:T(2,128)(2,1)S(1)} async-done(((bf16[128,33,2,128]{3,2,1,0:T(2,128)(2,1)}), bf16[128,33,2,128]{3,2,1,0:T(2,128)(2,1)S(1)}, u32[]{:S(2)}, u32[]{:S(2)}) %all-to-all-start) | async-done | bytes 2162720 | tf_op jit(solution)/shard_map/all_to_all | solution.py:458
  48.4 0.0 copy-done.1
  48.4 0.0 copy-done.2
  48.4 0.0 copy-done.3
  48.4 0.0 copy-done.4
  48.5 0.0 copy-done.5
  48.5 0.0 copy-done.6
  48.5 0.0 copy-done.8
  48.5 0.0 copy-done.9
  48.5 6.6 %spectral.1 = bf16[128,32,128]{2,1,0:T(8,128)(2,1)} custom-call(bf16[8448,128]{1,0:T(8,128)(2,1)S(1)} %bitcast.3, f32[3,128]{1,0:T(4,128)S(1)} %maximum_convert_fusion.taps_ref, bf16[256,128]{1,0:T(8,128)(2,1)S(1)} %copy-done.3, bf16[256,256]{1,0:T(8,128)(2,1)S(1)} %copy-done.1, bf16[256,256]{1,0:T(8,128)(2,1)S(1)} %copy-done.2, ...), custom_call_target="tpu_custom_call" | custom-call | tf_op jit(solution)/shard_map/spectral/pallas_call | solution.py:329
  55.1 4.7 %all-to-all-start.1 = ((bf16[128,32,128]{2,1,0:T(8,128)(2,1)}), bf16[128,32,128]{2,1,0:T(8,128)(2,1)S(1)}, u32[]{:S(2)}, u32[]{:S(2)}) async-start(bf16[128,32,128]{2,1,0:T(8,128)(2,1)} %spectral.1), calls=%async_computation.1 | async-start | bytes 2097152 | tf_op jit(solution)/shard_map/all_to_all | solution.py:463
  59.8 1.0 %slice.3 = bf16[2,12288]{1,0:T(2,128)(2,1)S(1)} slice(bf16[128,12288]{1,0:T(8,128)(2,1)} %v_ref.1), slice={[126:128], [0:12288]} | slice | bytes 98304 | tf_op jit(solution)/shard_map/slice | solution.py:460
  60.8 0.0 copy-start.7
  60.8 3.3 %collective-permute-start = (bf16[2,12288]{1,0:T(2,128)(2,1)S(1)}, bf16[2,12288]{1,0:T(2,128)(2,1)S(1)}, u32[]{:S(2)}, u32[]{:S(2)}) collective-permute-start(bf16[2,12288]{1,0:T(2,128)(2,1)S(1)} %slice.3), channel_id=1, source_target_pairs={{0,1},{1,2},{2,3},{3,4},{4,5},{5,6},{6,7},{7,8},{8,9},{9,10},{10,1... | collective-permute-start | bytes 147464 | tf_op jit(solution)/shard_map/ppermute | solution.py:460
  64.1 14.7 %collective-permute-done.rq_ref.rk_ref.rv_ref = bf16[2,12288]{1,0:T(2,128)(2,1)S(1)} collective-permute-done((bf16[2,12288]{1,0:T(2,128)(2,1)S(1)}, bf16[2,12288]{1,0:T(2,128)(2,1)S(1)}, u32[]{:S(2)}, u32[]{:S(2)}) %collective-permute-start) | collective-permute-done | bytes 49184 | tf_op jit(solution)/shard_map/ppermute | solution.py:460
  78.8 6.0 %side.1 = (bf16[128,4096]{1,0:T(8,128)(2,1)S(1)}, bf16[128,4096]{1,0:T(8,128)(2,1)S(1)}) custom-call(bf16[128,12288]{1,0:T(8,128)(2,1)} %v_ref.1, bf16[128,12288]{1,0:T(8,128)(2,1)} %v_ref.1, bf16[128,12288]{1,0:T(8,128)(2,1)} %v_ref.1, bf16[2,12288]{1,0:T(2,128)(2,1)S(1)} %collective-permute-done.rq_ref.rk_ref.rv_ref, ...), custom_call_target="tpu_custom_call" | custom-call | tf_op jit(solution)/shard_map/side/pallas_call | solution.py:425
  84.8 0.0 all-to-all-done.1.c_ref
  84.8 0.0 copy-done.7
  84.8 1.2 %mix.1 = bf16[128,4096]{1,0:T(8,128)(2,1)} custom-call(bf16[128,32,128]{2,1,0:T(8,128)(2,1)S(1)} %all-to-all-done.1.c_ref, bf16[128,4096]{1,0:T(8,128)(2,1)S(1)} %get-tuple-element.7.q_ref, f32[1,4096]{1,0:T(1,128)S(1)} %bitcast.4, bf16[128,4096]{1,0:T(8,128)(2,1)S(1)} %get-tuple-element.8.g_ref), custom_call_target="tpu_custom_call" | custom-call | tf_op jit(solution)/shard_map/mix/pallas_call | solution.py:381
Async XLA Ops:
  6.2 11.6 %copy-start = (bf16[3,12288]{1,0:T(4,128)(2,1)S(1)}, bf16[3,12288]{1,0:T(4,128)(2,1)}, u32[]{:S(2)}) copy-start(bf16[3,12288]{1,0:T(4,128)(2,1)} %wv_ref.1) | copy-start | bytes 221188
  6.2 42.3 %copy-start.1 = (bf16[256,256]{1,0:T(8,128)(2,1)S(1)}, bf16[256,256]{1,0:T(8,128)(2,1)}, u32[]{:S(2)}) copy-start(bf16[256,256]{1,0:T(8,128)(2,1)} %constant.41.clone.fwd_ref) | copy-start | bytes 393220
  6.2 42.2 %copy-start.2 = (bf16[256,256]{1,0:T(8,128)(2,1)S(1)}, bf16[256,256]{1,0:T(8,128)(2,1)}, u32[]{:S(2)}) copy-start(bf16[256,256]{1,0:T(8,128)(2,1)} %constant.42.clone.bwd_ref) | copy-start | bytes 393220
  6.2 42.2 %copy-start.3 = (bf16[256,128]{1,0:T(8,128)(2,1)S(1)}, bf16[256,128]{1,0:T(8,128)(2,1)}, u32[]{:S(2)}) copy-start(bf16[256,128]{1,0:T(8,128)(2,1)} %constant.40.clone.first_ref) | copy-start | bytes 196612
  6.2 42.2 %copy-start.4 = (bf16[128,256]{1,0:T(8,128)(2,1)S(1)}, bf16[128,256]{1,0:T(8,128)(2,1)}, u32[]{:S(2)}) copy-start(bf16[128,256]{1,0:T(8,128)(2,1)} %constant.43.clone.last_ref) | copy-start | bytes 196612
  6.2 42.2 %copy-start.5 = (f32[128,128]{1,0:T(8,128)S(1)}, f32[128,128]{1,0:T(8,128)}, u32[]{:S(2)}) copy-start(f32[128,128]{1,0:T(8,128)} %constant.44.clone.tc_ref) | copy-start | bytes 196612
  6.2 42.2 %copy-start.6 = (f32[128,128]{1,0:T(8,128)S(1)}, f32[128,128]{1,0:T(8,128)}, u32[]{:S(2)}) copy-start(f32[128,128]{1,0:T(8,128)} %constant.45.clone.ts_ref) | copy-start | bytes 196612
  6.3 42.2 %copy-start.8 = (f32[1,128]{1,0:T(1,128)S(1)}, f32[1,128]{1,0:T(1,128)}, u32[]{:S(2)}) copy-start(f32[1,128]{1,0:T(1,128)} %constant.46.clone.hc_ref) | copy-start | bytes 1540
  6.3 42.2 %copy-start.9 = (f32[1,128]{1,0:T(1,128)S(1)}, f32[1,128]{1,0:T(1,128)}, u32[]{:S(2)}) copy-start(f32[1,128]{1,0:T(1,128)} %constant.47.clone.hs_ref) | copy-start | bytes 1540
  6.3 42.2 %all-to-all-start = ((bf16[128,33,2,128]{3,2,1,0:T(2,128)(2,1)}), bf16[128,33,2,128]{3,2,1,0:T(2,128)(2,1)S(1)}, u32[]{:S(2)}, u32[]{:S(2)}) async-start(bf16[128,33,2,128]{3,2,1,0:T(2,128)(2,1)} %bitcast.5), calls=%async_computation | async-start | bytes 4325376 | tf_op jit(solution)/shard_map/all_to_all | solution.py:458
  55.1 29.7 %all-to-all-start.1 = ((bf16[128,32,128]{2,1,0:T(8,128)(2,1)}), bf16[128,32,128]{2,1,0:T(8,128)(2,1)S(1)}, u32[]{:S(2)}, u32[]{:S(2)}) async-start(bf16[128,32,128]{2,1,0:T(8,128)(2,1)} %spectral.1), calls=%async_computation.1 | async-start | bytes 2097152 | tf_op jit(solution)/shard_map/all_to_all | solution.py:463
  60.8 24.0 %copy-start.7 = (f32[4096]{0:T(1024)S(1)}, f32[4096]{0:T(1024)}, u32[]{:S(2)}) copy-start(f32[4096]{0:T(1024)} %param.15) | copy-start | bytes 49156
  60.8 18.0 %collective-permute-start = (bf16[2,12288]{1,0:T(2,128)(2,1)S(1)}, bf16[2,12288]{1,0:T(2,128)(2,1)S(1)}, u32[]{:S(2)}, u32[]{:S(2)}) collective-permute-start(bf16[2,12288]{1,0:T(2,128)(2,1)S(1)} %slice.3), channel_id=1, source_target_pairs={{0,1},{1,2},{2,3},{3,4},{4,5},{5,6},{6,7},{7,8},{8,9},{9,10},{10,1... | collective-permute-start | bytes 147464 | tf_op jit(solution)/shard_map/ppermute | solution.py:460

commit v7 on v6

--- a/solution.py
+++ b/solution.py
@@ -79,19 +79,20 @@
     ahead = 2
 
     def reads(i):
-        at = pl.ds(i * cols, cols)
+        start = pl.multiple_of(i * cols, cols)
+        at = pl.ds(start, cols)
         return (
             pltpu.make_async_copy(
-                p_ref.at[:, pl.ds(width + i * cols, cols)], k_buf.at[:, at], sem.at[i, 0]
+                p_ref.at[:, pl.ds(width + start, cols)], k_buf.at[:, at], sem.at[i, 0]
             ),
             pltpu.make_async_copy(
-                p_ref.at[:, pl.ds(2 * width + i * cols, cols)], v_buf.at[:, at], sem.at[i, 1]
+                p_ref.at[:, pl.ds(2 * width + start, cols)], v_buf.at[:, at], sem.at[i, 1]
             ),
             pltpu.make_async_copy(f_ref.at[:, at], f_buf.at[:, at], sem.at[i, 2]),
         )
 
     def write(i):
-        at = pl.ds(i * chunk, chunk)
+        at = pl.ds(pl.multiple_of(i * chunk, chunk), chunk)
         return pltpu.make_async_copy(out_buf.at[at], send_ref.at[at], sem.at[i, 3])
 
     taps_read = pltpu.make_async_copy(t_ref, w_ref, tap_sem)
@@ -106,18 +107,22 @@
     row = lax.broadcasted_iota(jnp.int32, (8, lanes), 0) % 4
     piece = lax.broadcasted_iota(jnp.int32, (8, lanes), 1) // own
     taps_read.wait()
-    for i in range(steps):
+
+    def turn(i, carry):
         for copy in reads(i):
             copy.wait()
-        if i + ahead < steps:
+
+        @pl.when(i + ahead < steps)
+        def _():
             for copy in reads(i + ahead):
                 copy.start()
+
         for j in range(cols // lanes):
-            start = i * cols + j * lanes
-            at = slice(start, start + lanes)
+            start = pl.multiple_of(i * cols + j * lanes, lanes)
+            at = pl.ds(start, lanes)
 
             def featurized(buf, ext, base):
-                taps = w_ref[:, base + start : base + start + lanes].astype(F32)
+                taps = w_ref[:, pl.ds(base + start, lanes)].astype(F32)
                 ext[j, lead:] = buf[:, at].astype(F32)
                 return (
                     taps[0:1] * ext[j, lead : lead + tok]
@@ -139,18 +144,25 @@
             for k in range(near):
                 to = (j * near + k) * run
                 mine = slice(k * own, (k + 1) * own)
-                stage[i % 2, to : to + own, :] = gated[mine]
-                stage[i % 2, to + own : to + 2 * own, :] = taken[mine]
+                stage[to : to + own, :] = gated[mine]
+                stage[to + own : to + 2 * own, :] = taken[mine]
                 part = pltpu.roll(turned, lanes - k * own, 1) if k else turned
                 part = jnp.where(row == piece, part, 0.0)
                 part = part + pltpu.roll(part, 7, 0)
                 part = part + pltpu.roll(part, 6, 0)
-                stage[i % 2, to + 2 * own : to + 2 * own + 1, :] = part[0:1]
-                stage[i % 2, to + 2 * own + 1 : to + 2 * own + 2, :] = part[4:5]
-        out_buf[i * chunk : (i + 1) * chunk] = stage[i % 2].astype(BF16)
+                stage[to + 2 * own : to + 2 * own + 1, :] = part[0:1]
+                stage[to + 2 * own + 1 : to + 2 * own + 2, :] = part[4:5]
+        out_buf[pl.ds(pl.multiple_of(i * chunk, chunk), chunk), :] = stage[...].astype(BF16)
         write(i).start()
-    for i in range(steps):
+        return carry
+
+    lax.fori_loop(0, steps, turn, 0)
+
+    def drain(i, carry):
         write(i).wait()
+        return carry
+
+    lax.fori_loop(0, steps, drain, 0)
 
 
 def gate(projected, short_filter, long_filter, devices):
@@ -173,7 +185,7 @@
             pltpu.VMEM((cols // 128, tok + 8, 128), F32),
             pltpu.VMEM((cols // 128, tok + 8, 128), F32),
             pltpu.VMEM((cols // 128, 8, 128), F32),
-            pltpu.VMEM((2, cols // own * run, 128), F32),
+            pltpu.VMEM((cols // own * run, 128), F32),
             pltpu.SemaphoreType.DMA((steps, 4)),
             pltpu.SemaphoreType.DMA(()),
         ],
@@ -227,7 +239,7 @@
     def first_row(row, block):
         return jnp.concatenate([jnp.where(index == 0, row, block[:top]), block[top:]], 0)
 
-    group, group2, group3, group4 = 16, 16, 16, 32
+    group, group2, group3, group4 = 16, 16, 16, 16
 
     run = 16
 
@@ -313,10 +325,14 @@
         at = pl.ds(i * piece, piece)
         return pltpu.make_async_copy(block_ref.at[at], out_ref.at[at], sem.at[i])
 
-    for i in range(segments // piece):
-        for b in range(i * piece, (i + 1) * piece):
-            block_ref[b] = conv_ref[b * out_pitch : b * out_pitch + own, :].astype(BF16)
+    def narrow(i, carry):
+        for j in range(piece):
+            b = i * piece + j
+            block_ref[b] = conv_ref[pl.ds(b * out_pitch, own), :].astype(BF16)
         write(i).start()
+        return carry
+
+    lax.fori_loop(0, segments // piece, narrow, 0)
     for i in range(segments // piece):
         write(i).wait()
 

time: 86.6 us -> 86.8 us (level)
  no operation moved by 1% of the time
where the time goes in v7:
time: 86.8 us; the launch traced here: 86.3 us
  waiting for transfers between devices  45.2 us (52%)
  Pallas kernels  20.2 us (23%)
  starting transfers between devices  19.5 us (22%)
  local copies, waits for them, and re-layouts  1.13 us (1%)
    all_to_all x1, waiting for transfers between devices, shards(): lax.all_to_all(pairs, TURNED, split_axis=0, concat_axis=0, tiled=True)  30.5 us
    ppermute x1, waiting for transfers between devices, shards(): lax.ppermute(projected[tok - rim_count:], AXES, [(i, i + 1) for i in rang...  14.7 us
    all_to_all x1, starting transfers between devices, shards(): lax.all_to_all(pairs, TURNED, split_axis=0, concat_axis=0, tiled=True)  11.5 us
    pallas_call x1, Pallas kernels, spectral(): pl.pallas_call(functools.partial(spectral_kernel, outer), out_shape=pltpu...  6.77 us
    pallas_call x1, Pallas kernels, gate(): pl.pallas_call(functools.partial(gate_kernel, own), in_specs=[pl.BlockSpe...  6.21 us
    pallas_call x1, Pallas kernels, side(): pl.pallas_call(side_kernel, grid=(steps,), in_specs=thirds(tok) + thirds(...  6 us
    all_to_all x1, starting transfers between devices, shards(): conv = lax.all_to_all(conv, TURNED, split_axis=0, concat_axis=0, tiled=True)  4.69 us
    ppermute x1, starting transfers between devices, shards(): lax.ppermute(projected[tok - rim_count:], AXES, [(i, i + 1) for i in rang...  3.28 us
  transfers between devices with their start and end apart: 3, of which 2 were waited for; matrix products, arithmetic and copies ran while one was open for 1% of the time, Pallas kernels for 7%

profile of v7, /device:TPU:1, one launch (start us, length us, event | category | flops | bytes accessed | tf_op | source)
XLA Modules:
  0.0 86.3 jit_solution(15158072048989145499)
XLA Ops:
  0.0 6.2 %gate.1 = bf16[8448,128]{1,0:T(8,128)(2,1)} custom-call(bf16[128,12288]{1,0:T(8,128)(2,1)} %v_ref.1, bf16[128,4096]{1,0:T(8,128)(2,1)} %f_ref.1, bf16[3,12288]{1,0:T(4,128)(2,1)} %wv_ref.1), custom_call_target="tpu_custom_call" | custom-call | tf_op jit(solution)/shard_map/gate/pallas_call | solution.py:174
  6.2 0.0 copy-start
  6.2 0.0 copy-start.1
  6.2 0.0 copy-start.2
  6.3 0.0 copy-start.3
  6.3 0.0 copy-start.4
  6.3 0.0 copy-start.5
  6.3 0.0 copy-start.6
  6.3 0.0 copy-start.8
  6.3 0.0 copy-start.9
  6.3 11.5 %all-to-all-start = ((bf16[128,33,2,128]{3,2,1,0:T(2,128)(2,1)}), bf16[128,33,2,128]{3,2,1,0:T(2,128)(2,1)S(1)}, u32[]{:S(2)}, u32[]{:S(2)}) async-start(bf16[128,33,2,128]{3,2,1,0:T(2,128)(2,1)} %bitcast.5), calls=%async_computation | async-start | bytes 4325376 | tf_op jit(solution)/shard_map/all_to_all | solution.py:474
  17.8 0.0 copy-done
  17.8 0.1 constant_dynamic-slice_fusion.1
  17.9 0.1 maximum_convert_fusion.taps_ref
  18.0 30.5 %all-to-all-done = bf16[128,33,2,128]{3,2,1,0:T(2,128)(2,1)S(1)} async-done(((bf16[128,33,2,128]{3,2,1,0:T(2,128)(2,1)}), bf16[128,33,2,128]{3,2,1,0:T(2,128)(2,1)S(1)}, u32[]{:S(2)}, u32[]{:S(2)}) %all-to-all-start) | async-done | bytes 2162720 | tf_op jit(solution)/shard_map/all_to_all | solution.py:474
  48.5 0.0 copy-done.1
  48.5 0.0 copy-done.2
  48.5 0.0 copy-done.3
  48.5 0.0 copy-done.4
  48.5 0.0 copy-done.5
  48.5 0.0 copy-done.6
  48.5 0.0 copy-done.8
  48.5 0.0 copy-done.9
  48.5 6.8 %spectral.1 = bf16[128,32,128]{2,1,0:T(8,128)(2,1)} custom-call(bf16[8448,128]{1,0:T(8,128)(2,1)S(1)} %bitcast.3, f32[3,128]{1,0:T(4,128)S(1)} %maximum_convert_fusion.taps_ref, bf16[256,128]{1,0:T(8,128)(2,1)S(1)} %copy-done.3, bf16[256,256]{1,0:T(8,128)(2,1)S(1)} %copy-done.1, bf16[256,256]{1,0:T(8,128)(2,1)S(1)} %copy-done.2, ...), custom_call_target="tpu_custom_call" | custom-call | tf_op jit(solution)/shard_map/spectral/pallas_call | solution.py:345
  55.3 4.7 %all-to-all-start.1 = ((bf16[128,32,128]{2,1,0:T(8,128)(2,1)}), bf16[128,32,128]{2,1,0:T(8,128)(2,1)S(1)}, u32[]{:S(2)}, u32[]{:S(2)}) async-start(bf16[128,32,128]{2,1,0:T(8,128)(2,1)} %spectral.1), calls=%async_computation.1 | async-start | bytes 2097152 | tf_op jit(solution)/shard_map/all_to_all | solution.py:479
  60.0 1.0 %slice.3 = bf16[2,12288]{1,0:T(2,128)(2,1)S(1)} slice(bf16[128,12288]{1,0:T(8,128)(2,1)} %v_ref.1), slice={[126:128], [0:12288]} | slice | bytes 98304 | tf_op jit(solution)/shard_map/slice | solution.py:476
  61.0 0.0 copy-start.7
  61.0 3.3 %collective-permute-start = (bf16[2,12288]{1,0:T(2,128)(2,1)S(1)}, bf16[2,12288]{1,0:T(2,128)(2,1)S(1)}, u32[]{:S(2)}, u32[]{:S(2)}) collective-permute-start(bf16[2,12288]{1,0:T(2,128)(2,1)S(1)} %slice.3), channel_id=1, source_target_pairs={{0,1},{1,2},{2,3},{3,4},{4,5},{5,6},{6,7},{7,8},{8,9},{9,10},{10,1... | collective-permute-start | bytes 147464 | tf_op jit(solution)/shard_map/ppermute | solution.py:476
  64.3 14.7 %collective-permute-done.rq_ref.rk_ref.rv_ref = bf16[2,12288]{1,0:T(2,128)(2,1)S(1)} collective-permute-done((bf16[2,12288]{1,0:T(2,128)(2,1)S(1)}, bf16[2,12288]{1,0:T(2,128)(2,1)S(1)}, u32[]{:S(2)}, u32[]{:S(2)}) %collective-permute-start) | collective-permute-done | bytes 49184 | tf_op jit(solution)/shard_map/ppermute | solution.py:476
  79.0 6.0 %side.1 = (bf16[128,4096]{1,0:T(8,128)(2,1)S(1)}, bf16[128,4096]{1,0:T(8,128)(2,1)S(1)}) custom-call(bf16[128,12288]{1,0:T(8,128)(2,1)} %v_ref.1, bf16[128,12288]{1,0:T(8,128)(2,1)} %v_ref.1, bf16[128,12288]{1,0:T(8,128)(2,1)} %v_ref.1, bf16[2,12288]{1,0:T(2,128)(2,1)S(1)} %collective-permute-done.rq_ref.rk_ref.rv_ref, ...), custom_call_target="tpu_custom_call" | custom-call | tf_op jit(solution)/shard_map/side/pallas_call | solution.py:441
  85.0 0.0 all-to-all-done.1.c_ref
  85.0 0.0 copy-done.7
  85.0 1.2 %mix.1 = bf16[128,4096]{1,0:T(8,128)(2,1)} custom-call(bf16[128,32,128]{2,1,0:T(8,128)(2,1)S(1)} %all-to-all-done.1.c_ref, bf16[128,4096]{1,0:T(8,128)(2,1)S(1)} %get-tuple-element.7.q_ref, f32[1,4096]{1,0:T(1,128)S(1)} %bitcast.4, bf16[128,4096]{1,0:T(8,128)(2,1)S(1)} %get-tuple-element.8.g_ref), custom_call_target="tpu_custom_call" | custom-call | tf_op jit(solution)/shard_map/mix/pallas_call | solution.py:397
Async XLA Ops:
  6.2 11.6 %copy-start = (bf16[3,12288]{1,0:T(4,128)(2,1)S(1)}, bf16[3,12288]{1,0:T(4,128)(2,1)}, u32[]{:S(2)}) copy-start(bf16[3,12288]{1,0:T(4,128)(2,1)} %wv_ref.1) | copy-start | bytes 221188
  6.2 42.3 %copy-start.1 = (bf16[256,256]{1,0:T(8,128)(2,1)S(1)}, bf16[256,256]{1,0:T(8,128)(2,1)}, u32[]{:S(2)}) copy-start(bf16[256,256]{1,0:T(8,128)(2,1)} %constant.41.clone.fwd_ref) | copy-start | bytes 393220
  6.2 42.2 %copy-start.2 = (bf16[256,256]{1,0:T(8,128)(2,1)S(1)}, bf16[256,256]{1,0:T(8,128)(2,1)}, u32[]{:S(2)}) copy-start(bf16[256,256]{1,0:T(8,128)(2,1)} %constant.42.clone.bwd_ref) | copy-start | bytes 393220
  6.3 42.2 %copy-start.3 = (bf16[256,128]{1,0:T(8,128)(2,1)S(1)}, bf16[256,128]{1,0:T(8,128)(2,1)}, u32[]{:S(2)}) copy-start(bf16[256,128]{1,0:T(8,128)(2,1)} %constant.40.clone.first_ref) | copy-start | bytes 196612
  6.3 42.2 %copy-start.4 = (bf16[128,256]{1,0:T(8,128)(2,1)S(1)}, bf16[128,256]{1,0:T(8,128)(2,1)}, u32[]{:S(2)}) copy-start(bf16[128,256]{1,0:T(8,128)(2,1)} %constant.43.clone.last_ref) | copy-start | bytes 196612
  6.3 42.2 %copy-start.5 = (f32[128,128]{1,0:T(8,128)S(1)}, f32[128,128]{1,0:T(8,128)}, u32[]{:S(2)}) copy-start(f32[128,128]{1,0:T(8,128)} %constant.44.clone.tc_ref) | copy-start | bytes 196612
  6.3 42.2 %copy-start.6 = (f32[128,128]{1,0:T(8,128)S(1)}, f32[128,128]{1,0:T(8,128)}, u32[]{:S(2)}) copy-start(f32[128,128]{1,0:T(8,128)} %constant.45.clone.ts_ref) | copy-start | bytes 196612
  6.3 42.2 %copy-start.8 = (f32[1,128]{1,0:T(1,128)S(1)}, f32[1,128]{1,0:T(1,128)}, u32[]{:S(2)}) copy-start(f32[1,128]{1,0:T(1,128)} %constant.46.clone.hc_ref) | copy-start | bytes 1540
  6.3 42.2 %copy-start.9 = (f32[1,128]{1,0:T(1,128)S(1)}, f32[1,128]{1,0:T(1,128)}, u32[]{:S(2)}) copy-start(f32[1,128]{1,0:T(1,128)} %constant.47.clone.hs_ref) | copy-start | bytes 1540
  6.3 42.2 %all-to-all-start = ((bf16[128,33,2,128]{3,2,1,0:T(2,128)(2,1)}), bf16[128,33,2,128]{3,2,1,0:T(2,128)(2,1)S(1)}, u32[]{:S(2)}, u32[]{:S(2)}) async-start(bf16[128,33,2,128]{3,2,1,0:T(2,128)(2,1)} %bitcast.5), calls=%async_computation | async-start | bytes 4325376 | tf_op jit(solution)/shard_map/all_to_all | solution.py:474
  55.3 29.7 %all-to-all-start.1 = ((bf16[128,32,128]{2,1,0:T(8,128)(2,1)}), bf16[128,32,128]{2,1,0:T(8,128)(2,1)S(1)}, u32[]{:S(2)}, u32[]{:S(2)}) async-start(bf16[128,32,128]{2,1,0:T(8,128)(2,1)} %spectral.1), calls=%async_computation.1 | async-start | bytes 2097152 | tf_op jit(solution)/shard_map/all_to_all | solution.py:479
  61.0 24.0 %copy-start.7 = (f32[4096]{0:T(1024)S(1)}, f32[4096]{0:T(1024)}, u32[]{:S(2)}) copy-start(f32[4096]{0:T(1024)} %param.15) | copy-start | bytes 49156
  61.0 18.0 %collective-permute-start = (bf16[2,12288]{1,0:T(2,128)(2,1)S(1)}, bf16[2,12288]{1,0:T(2,128)(2,1)S(1)}, u32[]{:S(2)}, u32[]{:S(2)}) collective-permute-start(bf16[2,12288]{1,0:T(2,128)(2,1)S(1)} %slice.3), channel_id=1, source_target_pairs={{0,1},{1,2},{2,3},{3,4},{4,5},{5,6},{6,7},{7,8},{8,9},{9,10},{10,1... | collective-permute-start | bytes 147464 | tf_op jit(solution)/shard_map/ppermute | solution.py:476
